TPU v7x, 256 devices: a whole 4x4x8 slice. The times are simulated.
256 devices in a mesh: xg: 4 (over x_hi, core), yd: 64 (over x_lo, z, y).
Axes of the slice: x: 4 (x_hi: 2, x_lo: 2; x = x_hi * 2 + x_lo), y: 4, z: 8, core: 2. Of those that a mesh axis runs over, the one named last changes fastest.
Arguments:
- mobile: float32 [4096, 1, 1024], P('yd', None, 'xg'), may hold values from 0 to 2
- dispersion_x: float32 [4096, 1, 1024], P('yd', None, 'xg'), may hold values from 0.5 to 200000
- dispersion_y: float32 [4096, 1, 1024], P('yd', None, 'xg'), may hold values from 0.5 to 200000
- capacity: float32 [4096, 1, 1024], P('yd', None, 'xg'), may hold values from 0.5 to 8
- immobile: float32 [4, 4096, 1, 1024], P(None, 'yd', None, 'xg'), may hold values from 0 to 2
- exchange_rates: float32 [4], replicated, may hold values from 0.02 to 50
- rate_shares: float32 [4], replicated, may hold values from 0.1 to 1
Outputs:
- updated: float32 [4096, 1, 1024], P('yd', None, 'xg')
All inputs are finite; a program needn't handle non-finite values.
Results may differ from a plain program's by a relative error of at most 0.0003.
Values sent between devices are 32-bit elements; how exact they have to be, the bound alone decides.
A program may use at most 64 MiB of HBM per device.

v0:
```python
import jax
import jax.numpy as jnp
from jax import lax
from jax.sharding import PartitionSpec as P


def shifted_2(value, axis, steps):
    count = lax.axis_size(axis)
    pairs = [(source, (source + steps) % count) for source in range(count)]
    return lax.ppermute(value, axis, pairs)


def shifted(values, stride, axis, filling):
    length = values.shape[axis]
    if stride > 0:
        kept_part = lax.slice_in_dim(values, 0, length - stride, axis=axis)
        filler = jnp.full_like(lax.slice_in_dim(values, 0, stride, axis=axis), filling)
        return jnp.concatenate([filler, kept_part], axis=axis)
    backward = -stride
    kept_part = lax.slice_in_dim(values, backward, length, axis=axis)
    filler = jnp.full_like(lax.slice_in_dim(values, 0, backward, axis=axis), filling)
    return jnp.concatenate([kept_part, filler], axis=axis)


def pick_at(values, position, axis):
    return lax.index_in_dim(values, position, axis, keepdims=False)


def periodic_solve(face_coef, storage, right_side, axis):
    length = right_side.shape[axis]
    sub_coef = -face_coef
    super_coef = -jnp.roll(face_coef, -1, axis)
    main_coef = storage + face_coef - super_coef
    stride = 1
    while stride < length // 2:
        sub_left = jnp.roll(sub_coef, stride, axis)
        main_left = jnp.roll(main_coef, stride, axis)
        super_left = jnp.roll(super_coef, stride, axis)
        side_left = jnp.roll(right_side, stride, axis)
        sub_right = jnp.roll(sub_coef, -stride, axis)
        main_right = jnp.roll(main_coef, -stride, axis)
        super_right = jnp.roll(super_coef, -stride, axis)
        side_right = jnp.roll(right_side, -stride, axis)
        left_ratio = sub_coef / main_left
        right_ratio = super_coef / main_right
        main_coef = main_coef - left_ratio * super_left - right_ratio * sub_right
        right_side = right_side - left_ratio * side_left - right_ratio * side_right
        sub_coef = -left_ratio * sub_left
        super_coef = -right_ratio * super_right
        stride = stride * 2
    coupling = sub_coef + super_coef
    main_other = jnp.roll(main_coef, stride, axis)
    coupling_other = jnp.roll(coupling, stride, axis)
    side_other = jnp.roll(right_side, stride, axis)
    return (right_side * main_other - coupling * side_other) / (
        main_coef * main_other - coupling * coupling_other
    )


def block_solve(face_coef, storage, source, axis):
    length = source.shape[axis]
    position = lax.broadcasted_iota(jnp.int32, source.shape, axis)
    at_first = position == 0
    at_last = position == length - 1
    following = shifted(face_coef, -1, axis, 0.0)
    nothing = jnp.zeros_like(source)
    sub_coef = jnp.where(at_first | at_last, nothing, -face_coef)
    super_coef = jnp.where(at_last, nothing, -following)
    main_coef = jnp.where(at_last, 1.0, storage + face_coef + following)
    right_side = jnp.stack(
        [
            jnp.where(at_last, nothing, source),
            jnp.where(at_first, face_coef, nothing),
            jnp.where(at_last, 1.0, nothing),
        ]
    )
    stride = 1
    while stride < length:
        sub_left = shifted(sub_coef, stride, axis, 0.0)
        main_left = shifted(main_coef, stride, axis, 1.0)
        super_left = shifted(super_coef, stride, axis, 0.0)
        side_left = shifted(right_side, stride, axis + 1, 0.0)
        sub_right = shifted(sub_coef, -stride, axis, 0.0)
        main_right = shifted(main_coef, -stride, axis, 1.0)
        super_right = shifted(super_coef, -stride, axis, 0.0)
        side_right = shifted(right_side, -stride, axis + 1, 0.0)
        left_ratio = sub_coef / main_left
        right_ratio = super_coef / main_right
        right_side = right_side - left_ratio[None] * side_left - right_ratio[None] * side_right
        main_coef = main_coef - left_ratio * super_left - right_ratio * sub_right
        sub_coef = -left_ratio * sub_left
        super_coef = -right_ratio * super_right
        stride = stride * 2
    return right_side / main_coef[None]


def reduced_rows(solved, face_coef, storage, source, upcoming, axis):
    from_next, face_next = upcoming
    length = source.shape[axis]
    face_last = pick_at(face_coef, length - 1, axis)
    sub_last = -face_last
    super_last = -face_next
    main_last = pick_at(storage, length - 1, axis) + face_last + face_next
    coef_prev = sub_last * pick_at(solved[1], length - 2, axis)
    coef_self = (
        main_last + sub_last * pick_at(solved[2], length - 2, axis) + super_last * from_next[1]
    )
    coef_next = super_last * from_next[2]
    target = (
        pick_at(source, length - 1, axis)
        - sub_last * pick_at(solved[0], length - 2, axis)
        - super_last * from_next[0]
    )
    return (coef_prev, coef_self, coef_next, target)


def dense_cyclic(all_rows, group_size):
    matrix_rows = []
    targets = []
    for row_index in range(group_size):
        entries = [jnp.zeros_like(all_rows[row_index, 1]) for column in range(group_size)]
        entries[(row_index - 1) % group_size] = all_rows[row_index, 0]
        entries[row_index] = all_rows[row_index, 1]
        entries[(row_index + 1) % group_size] = all_rows[row_index, 2]
        matrix_rows.append(entries)
        targets.append(all_rows[row_index, 3])
    for pivot in range(group_size):
        for row_index in range(pivot + 1, group_size):
            factor = matrix_rows[row_index][pivot] / matrix_rows[pivot][pivot]
            matrix_rows[row_index] = [
                matrix_rows[row_index][column] - factor * matrix_rows[pivot][column]
                for column in range(group_size)
            ]
            targets[row_index] = targets[row_index] - factor * targets[pivot]
    solutions = [None] * group_size
    for row_index in reversed(range(group_size)):
        total = targets[row_index]
        for column in range(row_index + 1, group_size):
            total = total - matrix_rows[row_index][column] * solutions[column]
        solutions[row_index] = total / matrix_rows[row_index][row_index]
    return jnp.stack(solutions)


def local(mobile, dispersion_x, dispersion_y, capacity, immobile, exchange_rates, rate_shares):
    weights = rate_shares * exchange_rates / (1.0 + exchange_rates)
    gain_terms = capacity[None] * weights[:, None, None, None]
    storage = 1.0 + jnp.sum(gain_terms, axis=0)
    source = mobile + jnp.sum(gain_terms * immobile, axis=0)
    solved = block_solve(dispersion_x, storage, source, 2)
    head_values = pick_at(solved, 0, 3)
    upcoming = shifted_2((head_values, pick_at(dispersion_x, 0, 2)), "xg", -1)
    rows = reduced_rows(solved, dispersion_x, storage, source, upcoming, 2)
    group_size = lax.axis_size("xg")
    all_rows = lax.all_gather(jnp.stack(rows)[None], "xg", axis=0, tiled=True)
    solutions = dense_cyclic(all_rows, group_size)
    own_index = lax.axis_index("xg")
    own_value = lax.dynamic_index_in_dim(solutions, own_index, 0, keepdims=False)
    prev_value = lax.dynamic_index_in_dim(
        solutions, (own_index + group_size - 1) % group_size, 0, keepdims=False
    )
    after_x = solved[0] + solved[1] * prev_value[..., None] + solved[2] * own_value[..., None]
    group_count = lax.axis_size("yd")

    def regroup(values):
        return values.reshape(values.shape[0], group_count, -1)

    line_values = lax.all_to_all(regroup(after_x), "yd", split_axis=1, concat_axis=0, tiled=True)
    line_faces = lax.all_to_all(
        regroup(dispersion_y), "yd", split_axis=1, concat_axis=0, tiled=True
    )
    line_storage = lax.all_to_all(regroup(storage), "yd", split_axis=1, concat_axis=0, tiled=True)
    solved_lines = periodic_solve(line_faces, line_storage, line_storage * line_values, 0)
    updated = lax.all_to_all(solved_lines, "yd", split_axis=0, concat_axis=1, tiled=True)
    updated = updated.reshape(after_x.shape)
    return updated


def solution(mesh):
    return jax.shard_map(
        local,
        mesh=mesh,
        in_specs=(
            P("yd", None, "xg"),
            P("yd", None, "xg"),
            P("yd", None, "xg"),
            P("yd", None, "xg"),
            P(None, "yd", None, "xg"),
            P(),
            P(),
        ),
        out_specs=P("yd", None, "xg"),
        check_vma=False,
    )
```

profile of v0, /device:TPU:2, one launch (start us, length us, event | category | flops | bytes accessed | tf_op | source)
XLA Modules:
  0.0 106.9 jit_solution(12925277914980473333)
XLA Ops:
  0.0 0.8 copy.95
  0.9 0.8 copy.55
  2.5 1.6 %fusion = (f32[64,256]{1,0:T(8,128)S(1)}, f32[64,256]{1,0:T(8,128)S(1)}) fusion(f32[4,64,1,256]{3,2,1,0:T(1,128)} %param.11, f32[64,256]{1,0:T(8,128)S(1)} %bitcast.400, f32[4]{0:T(128)S(1)} %add_divide_fusion), kind=kLoop, calls=%fused_computation.2 | loop fusion | flops 229376 | bytes 458768 | tf_op jit(solution)/shard_map/reduce_sum | solution.py:148
  4.1 0.9 add_select_fusion
  5.1 0.9 fusion.90
  11.7 1.6 %collective-permute-start.1 = (f32[3,64,1]{1,2,0:T(1,128)S(1)}, f32[3,64,1]{1,2,0:T(1,128)S(1)}, u32[]{:S(2)}, u32[]{:S(2)}) collective-permute-start(f32[3,64,1]{1,2,0:T(1,128)S(1)} %squeeze.95), channel_id=1, source_target_pairs={{0,192},{64,0},{128,64},{192,128},{1,193},{65,1},{129,65},{193,129... | collective-permute-start | bytes 2312 | tf_op jit(solution)/shard_map/ppermute | solution.py:10
  13.9 0.7 collective-permute-start
  14.7 0.8 reshape.21111
  15.5 13.2 %all-to-all-start.2 = ((f32[64,1,256]{2,1,0:T(1,128)}), f32[64,1,256]{2,1,0:T(1,128)S(1)}, u32[]{:S(2)}, u32[]{:S(2)}) async-start(f32[64,1,256]{2,1,0:T(1,128)} %reshape.21111), calls=%async_computation.2 | async-start | bytes 131072 | tf_op jit(solution)/shard_map/all_to_all | solution.py:168
  29.4 0.8 reshape.21113
  30.2 6.7 %all-gather = f32[16,64,1]{1,2,0:T(1,128)S(1)} all-gather(f32[4,64,1]{1,2,0:T(1,128)S(1)} %pad_maximum_fusion.2), channel_id=2, replica_groups=mesh['xg'=4,'yd'=64] {'xg'}, dimensions={0}, use_global_device_ids=true | all-gather | bytes 5120 | tf_op jit(solution)/shard_map/all_gather | solution.py:154
  37.1 0.8 reshape.21115
  38.1 11.0 %all-to-all-start = ((f32[64,1,256]{2,1,0:T(1,128)}), f32[64,1,256]{2,1,0:T(1,128)S(1)}, u32[]{:S(2)}, u32[]{:S(2)}) async-start(f32[64,1,256]{2,1,0:T(1,128)} %reshape.21113), calls=%async_computation | async-start | bytes 131072 | tf_op jit(solution)/shard_map/all_to_all | solution.py:171
  49.7 0.8 reduce.15
  50.8 7.7 %all-to-all-done = f32[64,1,256]{2,1,0:T(1,128)S(1)} async-done(((f32[64,1,256]{2,1,0:T(1,128)}), f32[64,1,256]{2,1,0:T(1,128)S(1)}, u32[]{:S(2)}, u32[]{:S(2)}) %all-to-all-start) | async-done | bytes 65568 | tf_op jit(solution)/shard_map/all_to_all | solution.py:171
  58.6 6.0 %all-to-all-start.1 = ((f32[64,1,256]{2,1,0:T(1,128)}), f32[64,1,256]{2,1,0:T(1,128)S(1)}, u32[]{:S(2)}, u32[]{:S(2)}) async-start(f32[64,1,256]{2,1,0:T(1,128)} %reshape.21115), calls=%async_computation.1 | async-start | bytes 131072 | tf_op jit(solution)/shard_map/all_to_all | solution.py:167
  64.5 0.8 reduce.14
  65.6 8.4 %all-to-all-done.1 = f32[64,1,256]{2,1,0:T(1,128)S(1)} async-done(((f32[64,1,256]{2,1,0:T(1,128)}), f32[64,1,256]{2,1,0:T(1,128)S(1)}, u32[]{:S(2)}, u32[]{:S(2)}) %all-to-all-start.1) | async-done | bytes 65568 | tf_op jit(solution)/shard_map/all_to_all | solution.py:167
  74.0 0.8 reduce.16
  84.9 1.7 %reshape.21117 = f32[64,1,256]{2,1,0:T(1,128)S(1)} reshape(f32[4096,4]{1,0:T(8,128)S(1)} %copy.96) | data formatting | bytes 131072
  86.6 14.6 %all_to_all.69 = f32[64,1,256]{2,1,0:T(1,128)S(1)} all-to-all(f32[64,1,256]{2,1,0:T(1,128)S(1)} %reshape.21117), channel_id=1, replica_groups=mesh['xg'=4,'yd'=64] {'yd'}, dimensions={0} | all-to-all | bytes 131072 | tf_op jit(solution)/shard_map/all_to_all | solution.py:173
  101.2 0.8 reduce.18
  102.0 3.4 %reshape.21118 = f32[4096,1,4]{2,1,0:T(1,128)S(1)} reshape(f32[64,256]{1,0:T(8,128)S(1)} %reduce.18) | data formatting | bytes 131072
  106.2 0.7 copy.85
  (228 shorter events, 19.4 us)
Async XLA Ops:
  0.0 6.0 %copy-start = (f32[64,1,256]{2,1,0:T(1,128)S(1)}, f32[64,1,256]{2,1,0:T(1,128)}, u32[]{:S(2)}) copy-start(f32[64,1,256]{2,1,0:T(1,128)} %param.8) | copy-start | bytes 196612
  11.1 3.5 %copy-start.1 = (f32[64,1,256]{2,1,0:T(1,128)S(1)}, f32[64,1,256]{2,1,0:T(1,128)}, u32[]{:S(2)}) copy-start(f32[64,1,256]{2,1,0:T(1,128)} %param.9) | copy-start | bytes 196612
  11.7 18.5 %collective-permute-start.1 = (f32[3,64,1]{1,2,0:T(1,128)S(1)}, f32[3,64,1]{1,2,0:T(1,128)S(1)}, u32[]{:S(2)}, u32[]{:S(2)}) collective-permute-start(f32[3,64,1]{1,2,0:T(1,128)S(1)} %squeeze.95), channel_id=1, source_target_pairs={{0,192},{64,0},{128,64},{192,128},{1,193},{65,1},{129,65},{193,129... | collective-permute-start | bytes 2312 | tf_op jit(solution)/shard_map/ppermute | solution.py:10
  13.9 16.3 %collective-permute-start = (f32[64,1]{0,1:T(1,128)S(1)}, f32[64,1]{0,1:T(1,128)S(1)}, u32[]{:S(2)}, u32[]{:S(2)}) collective-permute-start(f32[64,1]{0,1:T(1,128)S(1)} %bitcast.403), channel_id=1, source_target_pairs={{0,192},{64,0},{128,64},{192,128},{1,193},{65,1},{129,65},{193,129... | collective-permute-start | bytes 776 | tf_op jit(solution)/shard_map/ppermute | solution.py:10
  15.5 22.7 %all-to-all-start.2 = ((f32[64,1,256]{2,1,0:T(1,128)}), f32[64,1,256]{2,1,0:T(1,128)S(1)}, u32[]{:S(2)}, u32[]{:S(2)}) async-start(f32[64,1,256]{2,1,0:T(1,128)} %reshape.21111), calls=%async_computation.2 | async-start | bytes 131072 | tf_op jit(solution)/shard_map/all_to_all | solution.py:168
  38.1 20.4 %all-to-all-start = ((f32[64,1,256]{2,1,0:T(1,128)}), f32[64,1,256]{2,1,0:T(1,128)S(1)}, u32[]{:S(2)}, u32[]{:S(2)}) async-start(f32[64,1,256]{2,1,0:T(1,128)} %reshape.21113), calls=%async_computation | async-start | bytes 131072 | tf_op jit(solution)/shard_map/all_to_all | solution.py:171
  58.6 15.4 %all-to-all-start.1 = ((f32[64,1,256]{2,1,0:T(1,128)}), f32[64,1,256]{2,1,0:T(1,128)S(1)}, u32[]{:S(2)}, u32[]{:S(2)}) async-start(f32[64,1,256]{2,1,0:T(1,128)} %reshape.21115), calls=%async_computation.1 | async-start | bytes 131072 | tf_op jit(solution)/shard_map/all_to_all | solution.py:167
where the time goes:
time: 108 us; the launch traced here: 107 us
  starting transfers between devices  32.5 us (30%)
  local copies, waits for them, and re-layouts  21.3 us (20%)
  blocking collectives  21.3 us (20%)
  waiting for transfers between devices  16.5 us (15%)
  other arithmetic  14.1 us (13%)
  between operations  1.28 us (1%)
    all_to_all x1, blocking collectives, local(): lax.all_to_all(solved_lines, 'yd', split_axis=0, concat_axis=1, tiled=True)  14.6 us
    all_to_all x1, starting transfers between devices, local(): lax.all_to_all(regroup(dispersion_y), 'yd', split_axis=1, concat_axis=0,...  13.2 us
    all_to_all x1, starting transfers between devices, local(): lax.all_to_all(regroup(storage), 'yd', split_axis=1, concat_axis=0, tiled...  11 us
    unnamed x16, local copies, waits for them, and re-layouts  10.2 us
    all_to_all x1, waiting for transfers between devices, local(): lax.all_to_all(regroup(after_x), 'yd', split_axis=1, concat_axis=0, tiled...  8.39 us
    all_to_all x1, waiting for transfers between devices, local(): lax.all_to_all(regroup(storage), 'yd', split_axis=1, concat_axis=0, tiled...  7.73 us
    all_gather x1, blocking collectives, local(): all_rows = lax.all_gather(jnp.stack(rows)[None], 'xg', axis=0, tiled=True)  6.7 us
    all_to_all x1, starting transfers between devices, local(): lax.all_to_all(regroup(after_x), 'yd', split_axis=1, concat_axis=0, tiled...  5.96 us
  transfers between devices with their start and end apart: 5, of which 3 were waited for; matrix products, arithmetic and copies ran while one was open for 6% of the time, Pallas kernels for 0%

commit v1 on v0

v1 whole, which is shorter than its diff:
```python
import functools

import jax
import jax.numpy as jnp
from jax import lax
from jax.experimental import pallas as pl
from jax.experimental.pallas import tpu as pltpu
from jax.sharding import PartitionSpec as P

MESH = pl.DeviceIdType.MESH
Y_SIZE, Z_SIZE, XLO_SIZE, XG_SIZE = 4, 8, 2, 4
PLANE = XLO_SIZE * Y_SIZE
ROWS = 128
LANES = 128
SUB = 8

roll = pltpu.roll


def join_coef(left, right):
    e_a, gl_a, gr_a = left
    e_b, gl_b, gr_b = right
    ground = gr_a + gl_b
    inverse = 1.0 / (ground + (e_a + e_b))
    a = e_a * inverse
    b = e_b * inverse
    return (e_a * b, gl_a + a * ground, gr_b + b * ground), (a, b, inverse)


def join_side(left, right, factors):
    a, b, _ = factors
    middle = left[1] + right[0]
    return (left[0] + a * middle, right[1] + b * middle), middle


def between(factors, middle, u_left, u_right):
    a, b, inverse = factors
    return middle * inverse + a * u_left + b * u_right


def halves(values):
    count = values.shape[0]
    pairs = values.reshape((count // 2, 2) + values.shape[1:])
    return pairs[:, 0], pairs[:, 1]


def woven(first, second):
    count = first.shape[0]
    return jnp.stack([first, second], axis=1).reshape((2 * count,) + first.shape[1:])


def chain_coef(face, ground):
    (e_a, e_b), (g_a, g_b) = halves(face), halves(ground)
    inverse = 1.0 / (g_a + (e_a + e_b))
    a = e_a * inverse
    b = e_b * inverse
    coef = (e_a * b, a * g_a, g_b + b * g_a)
    saved = [(a, b, inverse)]
    while coef[0].shape[0] > 1:
        split = [halves(value) for value in coef]
        coef, factors = join_coef([s[0] for s in split], [s[1] for s in split])
        saved.append(factors)
    return tuple(value[0] for value in coef), saved


def chain_side(source, saved):
    f_a, f_b = halves(source)
    a, b, _ = saved[0]
    side = (a * f_a, f_b + b * f_a)
    middles = [f_a]
    for factors in saved[1:]:
        split = [halves(value) for value in side]
        side, middle = join_side([s[0] for s in split], [s[1] for s in split], factors)
        middles.append(middle)
    return tuple(value[0] for value in side), middles


def chain_back(saved, middles, u_left, u_right):
    u_left, u_right = u_left[None], u_right[None]
    for level in reversed(range(len(saved))):
        u_mid = between(saved[level], middles[level], u_left, u_right)
        if level:
            u_left, u_right = woven(u_left, u_mid), woven(u_mid, u_right)
        else:
            u_right = woven(u_mid, u_right)
    return u_right


def ahead(value, steps):
    return roll(value, value.shape[-2] - steps, value.ndim - 2)


def behind(value, steps):
    return roll(value, steps, value.ndim - 2)


def sub_coef(coef, steps):
    saved = []
    for step in steps:
        coef, factors = join_coef(coef, [ahead(value, step) for value in coef])
        saved.append(factors)
    return coef, saved


def sub_side(side, saved, steps):
    middles = []
    for step, factors in zip(steps, saved):
        side, middle = join_side(side, [ahead(value, step) for value in side], factors)
        middles.append(middle)
    return side, middles


def sub_back(saved, middles, steps, u_left, u_right):
    place = lax.broadcasted_iota(jnp.int32, u_left.shape, u_left.ndim - 2)
    for step, factors, middle in reversed(list(zip(steps, saved, middles))):
        u_mid = between(factors, middle, u_left, u_right)
        first = (place & step) == 0
        u_left, u_right = (
            jnp.where(first, u_left, behind(u_mid, step)),
            jnp.where(first, u_mid, behind(u_right, step)),
        )
    return u_left, u_right


def ring_coef(first, second):
    link = first[0] + second[0]
    ground_q = first[2] + second[1]
    ground_p = second[2] + first[1]
    inverse = 1.0 / (ground_q * ground_p + link * (ground_q + ground_p))
    link = link * inverse
    return link, ground_p * inverse + link, ground_q * inverse + link


def ring_solve(ring, first, second):
    link, to_q, to_p = ring
    f_q = first[1] + second[0]
    f_p = second[1] + first[0]
    return to_p * f_p + link * f_q, to_q * f_q + link * f_p


def strided(ref, stride):
    return jnp.stack([ref[pl.ds(start, SUB, stride=stride), :] for start in range(stride)])


def kernel(
    mobile_hbm, dx_hbm, dy_hbm, cap_hbm, imm_hbm, rates_ref, shares_ref, out_ref,
    mobile_ref, dx_ref, dy_ref, cap_ref, imm_ref, sto_ref, work_ref, work2_ref,
    x_ref, pc_ref, pr_ref, zc_ref, zr_ref, pick_ref,
    in_sem, x_send, x_recv, pc_send, pc_recv, pr_send, pr_recv,
    zc_send, zc_recv, zr_send, zr_recv,
):
    xg = lax.axis_index("xg")
    yd = lax.axis_index("yd")
    xlo = yd // (Z_SIZE * Y_SIZE)
    zz = (yd // Y_SIZE) % Z_SIZE
    yy = yd % Y_SIZE
    slot = xlo * Y_SIZE + yy

    loads = [
        pltpu.make_async_copy(src, dst, in_sem.at[i])
        for i, (src, dst) in enumerate(
            [(imm_hbm, imm_ref), (cap_hbm, cap_ref), (mobile_hbm, mobile_ref), (dx_hbm, dx_ref), (dy_hbm, dy_ref)]
        )
    ]
    for load in loads:
        load.start()

    x_peers = [{"xg": (xg + k) % XG_SIZE, "yd": yd} for k in range(1, XG_SIZE)]
    plane_peers = []
    for k in range(1, PLANE):
        other = (slot + k) % PLANE
        plane_peers.append({"xg": xg, "yd": (other // Y_SIZE) * (Z_SIZE * Y_SIZE) + zz * Y_SIZE + other % Y_SIZE})
    z_peers = [
        {"xg": xg, "yd": xlo * (Z_SIZE * Y_SIZE) + ((zz + k) % Z_SIZE) * Y_SIZE + yy} for k in range(1, Z_SIZE)
    ]
    barrier = pltpu.get_barrier_semaphore()
    for peer in z_peers + plane_peers + x_peers:
        pl.semaphore_signal(barrier, inc=1, device_id=peer, device_id_type=MESH)

    def sends(ref, rows, position, peers, send_sem, recv_sem):
        part = ref.at[pl.ds(pl.multiple_of(position * rows, rows), rows)]
        return [
            pltpu.make_async_remote_copy(
                src_ref=part, dst_ref=part, send_sem=send_sem.at[k], recv_sem=recv_sem.at[k],
                device_id=peer, device_id_type=MESH,
            )
            for k, peer in enumerate(peers)
        ]

    weights = []
    for k in range(4):
        rate = jnp.full((SUB, LANES), rates_ref[k], jnp.float32)
        weights.append(rate * jnp.full((SUB, LANES), shares_ref[k], jnp.float32) / (1.0 + rate))
    loads[0].wait()
    loads[1].wait()
    loads[2].wait()
    capacity = cap_ref[...].reshape(16, SUB, LANES)
    imm = imm_ref[...].reshape(4, 16, SUB, LANES)
    storage = 1.0 + capacity * (weights[0] + weights[1] + weights[2] + weights[3])
    mixed = weights[0] * imm[0] + weights[1] * imm[1] + weights[2] * imm[2] + weights[3] * imm[3]
    source = mobile_ref[...].reshape(16, SUB, LANES) + capacity * mixed
    storage = storage.reshape(ROWS, LANES)
    sto_ref[...] = storage

    loads[3].wait()
    work_ref[...] = jnp.transpose(dx_ref[...])
    work2_ref[...] = jnp.transpose(storage)
    x_coef, x_saved = chain_coef(strided(work_ref, 16), strided(work2_ref, 16))
    work_ref[...] = jnp.transpose(source.reshape(ROWS, LANES))
    x_side, x_mid = chain_side(strided(work_ref, 16), x_saved)
    steps = (1, 2, 4)
    x_coef, xs_saved = sub_coef(x_coef, steps)
    x_side, xs_mid = sub_side(x_side, xs_saved, steps)
    for k, value in enumerate(x_coef + x_side):
        x_ref[0, pl.ds(k, 1), :] = value[0:1]

    loads[4].wait()
    y_face = strided(dy_ref, 16).reshape(8, 2, SUB, LANES)
    y_ground = strided(sto_ref, 16).reshape(8, 2, SUB, LANES)
    y_coef, y_saved = chain_coef(y_face, y_ground)
    y_coef, ys_saved = sub_coef(y_coef, steps)
    base = pl.multiple_of(slot * 8, 8)
    for k in range(3):
        for t in range(2):
            pc_ref[pl.ds(base + 2 * k + t, 1), :] = y_coef[k][t, 0:1]

    pl.semaphore_wait(barrier, len(z_peers + plane_peers + x_peers))

    x_copies = [
        pltpu.make_async_remote_copy(
            src_ref=x_ref.at[0], dst_ref=x_ref.at[XG_SIZE - k], send_sem=x_send.at[k - 1],
            recv_sem=x_recv.at[k - 1], device_id=x_peers[k - 1], device_id_type=MESH,
        )
        for k in range(1, XG_SIZE)
    ]
    for copy in x_copies:
        copy.start()
    pc_copies = sends(pc_ref, 8, slot, plane_peers, pc_send, pc_recv)
    for copy in pc_copies:
        copy.start()

    for copy in x_copies:
        copy.wait()

    def next_lane(value):
        return roll(value, LANES - 1, 1)

    def block(g):
        rows = [x_ref[g, pl.ds(k, 1), :] for k in range(5)]
        rows = [jnp.broadcast_to(row, (SUB, LANES)) for row in rows]
        later = [next_lane(row) for row in rows]
        coef, factors = join_coef(rows[:3], later[:3])
        side, middle = join_side(rows[3:], later[3:], factors)
        return coef, side, factors, middle

    own_coef, own_side, own_factors, own_middle = block(0)
    rest_coef, rest_side, _, _ = block(1)
    for g in (2, 3):
        coef, side, _, _ = block(g)
        rest_coef, factors = join_coef(rest_coef, coef)
        rest_side, _ = join_side(rest_side, side, factors)
    u_before, u_last = ring_solve(ring_coef(own_coef, rest_coef), own_side, rest_side)
    u_half = between(own_factors, own_middle, u_before, u_last)
    even = (lax.broadcasted_iota(jnp.int32, (SUB, LANES), 1) & 1) == 0
    u_left = jnp.where(even, u_before, roll(u_half, 1, 1))
    u_right = jnp.where(even, u_half, roll(u_last, 1, 1))
    u_left, u_right = sub_back(xs_saved, xs_mid, steps, u_left, u_right)
    after_x = chain_back(x_saved, x_mid, u_left, u_right)
    for v in range(16):
        work_ref[pl.ds(v, SUB, stride=16), :] = after_x[v]
    work2_ref[...] = jnp.transpose(work_ref[...]) * sto_ref[...]

    y_side, y_mid = chain_side(strided(work2_ref, 16).reshape(8, 2, SUB, LANES), y_saved)
    y_side, ys_mid = sub_side(y_side, ys_saved, steps)
    for k in range(2):
        for t in range(2):
            pr_ref[pl.ds(base + 2 * k + t, 1), :] = y_side[k][t, 0:1]
    pr_copies = sends(pr_ref, 8, slot, plane_peers, pr_send, pr_recv)
    for copy in pr_copies:
        copy.start()

    for copy in pc_copies:
        copy.wait()

    def plane_rows(ref, k):
        return jnp.stack([ref[pl.ds(2 * k + t, PLANE, stride=8), :] for t in range(2)])

    p_steps = (1, 2)
    p_coef, p_saved = sub_coef([plane_rows(pc_ref, k) for k in range(3)], p_steps)
    z_base = pl.multiple_of(zz * 16, 16)
    for h in range(2):
        for k in range(3):
            for t in range(2):
                zc_ref[pl.ds(z_base + 8 * h + 2 * k + t, 1), :] = p_coef[k][t, 4 * h : 4 * h + 1]
    zc_copies = sends(zc_ref, 16, zz, z_peers, zc_send, zc_recv)
    for copy in zc_copies:
        copy.start()

    for copy in pr_copies:
        copy.wait()
    p_side, p_mid = sub_side([plane_rows(pr_ref, k) for k in range(2)], p_saved, p_steps)
    r_base = pl.multiple_of(zz * 8, 8)
    for h in range(2):
        for k in range(2):
            for t in range(2):
                zr_ref[pl.ds(r_base + 4 * h + 2 * k + t, 1), :] = p_side[k][t, 4 * h : 4 * h + 1]
    zr_copies = sends(zr_ref, 8, zz, z_peers, zr_send, zr_recv)
    for copy in zr_copies:
        copy.start()

    for copy in zc_copies:
        copy.wait()

    def z_rows(ref, stride, half_rows, k):
        return jnp.stack(
            [
                jnp.stack([ref[pl.ds(half_rows * h + 2 * k + t, Z_SIZE, stride=stride), :] for t in range(2)])
                for h in range(2)
            ]
        )

    z_coef, z_saved = sub_coef([z_rows(zc_ref, 16, 8, k) for k in range(3)], steps)
    z_ring = ring_coef([value[0] for value in z_coef], [value[1] for value in z_coef])

    for copy in zr_copies:
        copy.wait()
    z_side, z_mid = sub_side([z_rows(zr_ref, 8, 4, k) for k in range(2)], z_saved, steps)
    u_p, u_q = ring_solve(z_ring, [value[0] for value in z_side], [value[1] for value in z_side])

    def spread(value):
        return jnp.broadcast_to(value[:, 0:1], value.shape)

    def picked(u_left, u_right, place):
        for i, value in enumerate((u_left, u_right)):
            for t in range(2):
                pick_ref[i, t] = value[t]
        return tuple(
            jnp.stack([pick_ref[i, t, pl.ds(place, SUB, stride=0), :] for t in range(2)]) for i in range(2)
        )

    lower = xlo == 0
    u_p, u_q = spread(u_p), spread(u_q)
    u_left, u_right = jnp.where(lower, u_p, u_q), jnp.where(lower, u_q, u_p)
    own_saved = [tuple(jnp.where(lower, value[0], value[1]) for value in factors) for factors in z_saved]
    own_mid = [jnp.where(lower, value[0], value[1]) for value in z_mid]
    u_left, u_right = sub_back(own_saved, own_mid, steps, u_left, u_right)
    u_left, u_right = picked(u_left, u_right, zz)
    u_left, u_right = sub_back(p_saved, p_mid, p_steps, u_left, u_right)
    u_left, u_right = picked(u_left, u_right, slot)
    u_left, u_right = sub_back(ys_saved, ys_mid, steps, u_left, u_right)
    updated = chain_back(y_saved, y_mid, u_left, u_right)
    for v in range(8):
        for t in range(2):
            out_ref[pl.ds(2 * v + t, SUB, stride=16), :] = updated[v, t]


def local(mobile, dispersion_x, dispersion_y, capacity, immobile, exchange_rates, rate_shares):
    flat = [value.reshape(ROWS, LANES) for value in (mobile, dispersion_x, dispersion_y, capacity)]
    any_spec = pl.BlockSpec(memory_space=pl.ANY)
    smem_spec = pl.BlockSpec(memory_space=pltpu.SMEM)
    square = pltpu.VMEM((ROWS, LANES), jnp.float32)
    dma = pltpu.SemaphoreType.DMA
    updated = pl.pallas_call(
        kernel,
        out_shape=jax.ShapeDtypeStruct((ROWS, LANES), jnp.float32),
        in_specs=[any_spec] * 5 + [smem_spec] * 2,
        out_specs=pl.BlockSpec(memory_space=pltpu.VMEM),
        scratch_shapes=[
            square, square, square, square, pltpu.VMEM((4 * ROWS, LANES), jnp.float32), square, square, square,
            pltpu.VMEM((XG_SIZE, 8, LANES), jnp.float32),
            pltpu.VMEM((PLANE * 8, LANES), jnp.float32),
            pltpu.VMEM((PLANE * 8, LANES), jnp.float32),
            pltpu.VMEM((Z_SIZE * 16, LANES), jnp.float32),
            pltpu.VMEM((Z_SIZE * 8, LANES), jnp.float32),
            pltpu.VMEM((2, 2, SUB, LANES), jnp.float32),
            dma((5,)),
            dma((XG_SIZE - 1,)), dma((XG_SIZE - 1,)),
            dma((PLANE - 1,)), dma((PLANE - 1,)), dma((PLANE - 1,)), dma((PLANE - 1,)),
            dma((Z_SIZE - 1,)), dma((Z_SIZE - 1,)), dma((Z_SIZE - 1,)), dma((Z_SIZE - 1,)),
        ],
        compiler_params=pltpu.CompilerParams(collective_id=0, has_side_effects=True),
    )(*flat, immobile.reshape(4 * ROWS, LANES), exchange_rates, rate_shares)
    return updated.reshape(mobile.shape)


def solution(mesh):
    return jax.shard_map(
        local,
        mesh=mesh,
        in_specs=(
            P("yd", None, "xg"),
            P("yd", None, "xg"),
            P("yd", None, "xg"),
            P("yd", None, "xg"),
            P(None, "yd", None, "xg"),
            P(),
            P(),
        ),
        out_specs=P("yd", None, "xg"),
        check_vma=False,
    )
```

time: 108 us -> 24.4 us (0.23)
  starting transfers between devices: 32.5 us -> 0 us
  Pallas kernels: 0 us -> 22.7 us
  blocking collectives: 21.3 us -> 0 us
  local copies, waits for them, and re-layouts: 21.3 us -> 1.47 us
  waiting for transfers between devices: 16.5 us -> 0 us
  other arithmetic: 14.1 us -> 0 us
  between operations: 1.28 us -> 0.01 us
    all_to_all x3 -> x0, starting transfers between devices: 30.1 us -> none  [the longest x1 13.2 us: local(): lax.all_to_all(regroup(dispersion_y), 'yd', split_axis=1, concat_axis=0,...]
    pallas_call x0 -> x1, Pallas kernels: none -> 22.7 us  [local(): pl.pallas_call(kernel, out_shape=jax.ShapeDtypeStruct((ROWS, LANES), jnp....]
    all_to_all x3 -> x0, waiting for transfers between devices: 16.5 us -> none  [the longest x1 8.39 us: local(): lax.all_to_all(regroup(after_x), 'yd', split_axis=1, concat_axis=0, tiled...]
    all_to_all x1 -> x0, blocking collectives: 14.6 us -> none  [local(): lax.all_to_all(solved_lines, 'yd', split_axis=0, concat_axis=1, tiled=True)]
    unnamed x16 -> x1, local copies, waits for them, and re-layouts: 10.2 us -> 1.47 us
    slice x131 -> x0, local copies, waits for them, and re-layouts: 8.52 us -> none  [the longest x23 1.88 us: shifted(): kept_part = lax.slice_in_dim(values, 0, length - stride, axis=axis)]
    all_gather x1 -> x0, blocking collectives: 6.7 us -> none  [local(): all_rows = lax.all_gather(jnp.stack(rows)[None], 'xg', axis=0, tiled=True)]
    sub x37 -> x0, other arithmetic: 4.54 us -> none  [the longest x11 1.75 us: periodic_solve(): right_side = right_side - left_ratio * side_left - right_ratio * side_right]
  transfers between devices with their start and end apart: 5 -> 0, of which waited for: 3 -> 0; matrix products, arithmetic and copies ran while one was open for 6% -> 0% of each run, Pallas kernels for 0% -> 0%
where the time goes in v1:
time: 24.4 us; the launch traced here: 24.2 us
  Pallas kernels  22.7 us (93%)
  local copies, waits for them, and re-layouts  1.47 us (6%)
    pallas_call x1, Pallas kernels, local(): pl.pallas_call(kernel, out_shape=jax.ShapeDtypeStruct((ROWS, LANES), jnp....  22.7 us
    unnamed x1, local copies, waits for them, and re-layouts  1.47 us

profile of v1, /device:TPU:2, one launch (start us, length us, event | category | flops | bytes accessed | tf_op | source)
XLA Modules:
  0.0 24.2 jit_solution(17226018337098690414)
XLA Ops:
  0.0 22.7 %shard_map.73 = f32[128,128]{1,0:T(8,128)} custom-call(f32[128,128]{1,0:T(8,128)} %bitcast.8, f32[128,128]{1,0:T(8,128)} %bitcast.9, f32[128,128]{1,0:T(8,128)} %bitcast.10, f32[128,128]{1,0:T(8,128)} %bitcast.11, f32[512,128]{1,0:T(8,128)} %bitcast.7, f32[4]{0:T(128)} %rates_ref.1, f32[4]{0:T(128)} %shares_ref.1), custom_call_target="tpu_custom_call" | custom-call | tf_op jit(solution)/shard_map/pallas_call | solution.py:363
  22.7 1.5 %copy.10 = f32[64,1,256]{2,1,0:T(1,128)} copy(f32[64,1,256]{2,1,0:T(1,128)} %bitcast.6) | data formatting | bytes 131072

commit v2 on v1

--- a/solution.py
+++ b/solution.py
@@ -143,11 +143,11 @@
 
 
 def kernel(
-    mobile_hbm, dx_hbm, dy_hbm, cap_hbm, imm_hbm, rates_ref, shares_ref, out_ref,
-    mobile_ref, dx_ref, dy_ref, cap_ref, imm_ref, sto_ref, work_ref, work2_ref,
-    x_ref, pc_ref, pr_ref, zc_ref, zr_ref, pick_ref,
+    mobile_hbm, dx_hbm, dy_hbm, cap_hbm, imm_hbm, rates_hbm, shares_hbm, out_ref,
+    mobile_ref, dx_ref, dy_ref, cap_ref, imm_ref, rates_ref, shares_ref, sto_ref, work_ref, work2_ref,
+    x_ref, pc_ref, pr_ref, zc_ref, part_ref, parts_ref, sums_ref, pick_ref,
     in_sem, x_send, x_recv, pc_send, pc_recv, pr_send, pr_recv,
-    zc_send, zc_recv, zr_send, zr_recv,
+    zc_send, zc_recv, part_send, part_recv, ready,
 ):
     xg = lax.axis_index("xg")
     yd = lax.axis_index("yd")
@@ -159,7 +159,10 @@
     loads = [
         pltpu.make_async_copy(src, dst, in_sem.at[i])
         for i, (src, dst) in enumerate(
-            [(imm_hbm, imm_ref), (cap_hbm, cap_ref), (mobile_hbm, mobile_ref), (dx_hbm, dx_ref), (dy_hbm, dy_ref)]
+            [
+                (rates_hbm, rates_ref), (shares_hbm, shares_ref), (cap_hbm, cap_ref), (dy_hbm, dy_ref),
+                (dx_hbm, dx_ref), (imm_hbm, imm_ref), (mobile_hbm, mobile_ref),
+            ]
         )
     ]
     for load in loads:
@@ -170,15 +173,14 @@
     for k in range(1, PLANE):
         other = (slot + k) % PLANE
         plane_peers.append({"xg": xg, "yd": (other // Y_SIZE) * (Z_SIZE * Y_SIZE) + zz * Y_SIZE + other % Y_SIZE})
-    z_peers = [
-        {"xg": xg, "yd": xlo * (Z_SIZE * Y_SIZE) + ((zz + k) % Z_SIZE) * Y_SIZE + yy} for k in range(1, Z_SIZE)
-    ]
+    plane_starts = [((zz + k) % Z_SIZE) * Y_SIZE for k in (4, 3, 5, 2, 6, 1, 7)]
+    z_peers = [{"xg": xg, "yd": xlo * (Z_SIZE * Y_SIZE) + start + yy} for start in plane_starts]
     barrier = pltpu.get_barrier_semaphore()
     for peer in z_peers + plane_peers + x_peers:
         pl.semaphore_signal(barrier, inc=1, device_id=peer, device_id_type=MESH)
 
-    def sends(ref, rows, position, peers, send_sem, recv_sem):
-        part = ref.at[pl.ds(pl.multiple_of(position * rows, rows), rows)]
+    def sends(ref, position, peers, send_sem, recv_sem):
+        part = ref.at[position]
         return [
             pltpu.make_async_remote_copy(
                 src_ref=part, dst_ref=part, send_sem=send_sem.at[k], recv_sem=recv_sem.at[k],
@@ -187,42 +189,43 @@
             for k, peer in enumerate(peers)
         ]
 
+    loads[0].wait()
+    loads[1].wait()
     weights = []
     for k in range(4):
         rate = jnp.full((SUB, LANES), rates_ref[k], jnp.float32)
         weights.append(rate * jnp.full((SUB, LANES), shares_ref[k], jnp.float32) / (1.0 + rate))
-    loads[0].wait()
-    loads[1].wait()
     loads[2].wait()
     capacity = cap_ref[...].reshape(16, SUB, LANES)
-    imm = imm_ref[...].reshape(4, 16, SUB, LANES)
     storage = 1.0 + capacity * (weights[0] + weights[1] + weights[2] + weights[3])
-    mixed = weights[0] * imm[0] + weights[1] * imm[1] + weights[2] * imm[2] + weights[3] * imm[3]
-    source = mobile_ref[...].reshape(16, SUB, LANES) + capacity * mixed
     storage = storage.reshape(ROWS, LANES)
     sto_ref[...] = storage
 
+    steps = (1, 2, 4)
     loads[3].wait()
+    y_face = strided(dy_ref, 16).reshape(8, 2, SUB, LANES)
+    y_ground = strided(sto_ref, 16).reshape(8, 2, SUB, LANES)
+    y_coef, y_saved = chain_coef(y_face, y_ground)
+    y_coef, ys_saved = sub_coef(y_coef, steps)
+    for k in range(3):
+        for t in range(2):
+            pc_ref[slot, pl.ds(2 * k + t, 1), :] = y_coef[k][t, 0:1]
+
+    loads[4].wait()
     work_ref[...] = jnp.transpose(dx_ref[...])
     work2_ref[...] = jnp.transpose(storage)
     x_coef, x_saved = chain_coef(strided(work_ref, 16), strided(work2_ref, 16))
+    loads[5].wait()
+    loads[6].wait()
+    imm = imm_ref[...].reshape(4, 16, SUB, LANES)
+    mixed = weights[0] * imm[0] + weights[1] * imm[1] + weights[2] * imm[2] + weights[3] * imm[3]
+    source = mobile_ref[...].reshape(16, SUB, LANES) + capacity * mixed
     work_ref[...] = jnp.transpose(source.reshape(ROWS, LANES))
     x_side, x_mid = chain_side(strided(work_ref, 16), x_saved)
-    steps = (1, 2, 4)
     x_coef, xs_saved = sub_coef(x_coef, steps)
     x_side, xs_mid = sub_side(x_side, xs_saved, steps)
     for k, value in enumerate(x_coef + x_side):
         x_ref[0, pl.ds(k, 1), :] = value[0:1]
-
-    loads[4].wait()
-    y_face = strided(dy_ref, 16).reshape(8, 2, SUB, LANES)
-    y_ground = strided(sto_ref, 16).reshape(8, 2, SUB, LANES)
-    y_coef, y_saved = chain_coef(y_face, y_ground)
-    y_coef, ys_saved = sub_coef(y_coef, steps)
-    base = pl.multiple_of(slot * 8, 8)
-    for k in range(3):
-        for t in range(2):
-            pc_ref[pl.ds(base + 2 * k + t, 1), :] = y_coef[k][t, 0:1]
 
     pl.semaphore_wait(barrier, len(z_peers + plane_peers + x_peers))
 
@@ -233,14 +236,14 @@
         )
         for k in range(1, XG_SIZE)
     ]
+    pc_copies = sends(pc_ref, slot, plane_peers, pc_send, pc_recv)
+    for copy in x_copies + pc_copies:
+        copy.start()
+    for peer in z_peers:
+        pl.semaphore_signal(ready, inc=1, device_id=peer, device_id_type=MESH)
+
     for copy in x_copies:
-        copy.start()
-    pc_copies = sends(pc_ref, 8, slot, plane_peers, pc_send, pc_recv)
-    for copy in pc_copies:
-        copy.start()
-
-    for copy in x_copies:
-        copy.wait()
+        copy.wait_recv()
 
     def next_lane(value):
         return roll(value, LANES - 1, 1)
@@ -274,69 +277,94 @@
     y_side, ys_mid = sub_side(y_side, ys_saved, steps)
     for k in range(2):
         for t in range(2):
-            pr_ref[pl.ds(base + 2 * k + t, 1), :] = y_side[k][t, 0:1]
-    pr_copies = sends(pr_ref, 8, slot, plane_peers, pr_send, pr_recv)
+            pr_ref[slot, pl.ds(2 * k + t, 1), :] = y_side[k][t, 0:1]
+    pr_copies = sends(pr_ref, slot, plane_peers, pr_send, pr_recv)
     for copy in pr_copies:
         copy.start()
 
     for copy in pc_copies:
-        copy.wait()
+        copy.wait_recv()
 
     def plane_rows(ref, k):
-        return jnp.stack([ref[pl.ds(2 * k + t, PLANE, stride=8), :] for t in range(2)])
+        flat = ref.reshape(PLANE * 8, LANES)
+        return jnp.stack([flat[pl.ds(2 * k + t, PLANE, stride=8), :] for t in range(2)])
+
+    def at_row(value, place):
+        for t in range(2):
+            pick_ref[t] = value[t]
+        return jnp.stack([pick_ref[t, pl.ds(place, SUB, stride=0), :] for t in range(2)])
 
     p_steps = (1, 2)
     p_coef, p_saved = sub_coef([plane_rows(pc_ref, k) for k in range(3)], p_steps)
-    z_base = pl.multiple_of(zz * 16, 16)
     for h in range(2):
         for k in range(3):
             for t in range(2):
-                zc_ref[pl.ds(z_base + 8 * h + 2 * k + t, 1), :] = p_coef[k][t, 4 * h : 4 * h + 1]
-    zc_copies = sends(zc_ref, 16, zz, z_peers, zc_send, zc_recv)
+                zc_ref[zz, pl.ds(8 * h + 2 * k + t, 1), :] = p_coef[k][t, 4 * h : 4 * h + 1]
+    zc_copies = sends(zc_ref, zz, z_peers, zc_send, zc_recv)
     for copy in zc_copies:
         copy.start()
 
+    place = lax.broadcasted_iota(jnp.int32, (2, SUB, LANES), 1)
+    unit = jnp.where(place == slot, 1.0, 0.0)
+    zero = jnp.zeros_like(unit)
+    from_left, _ = sub_side((unit, zero), p_saved, p_steps)
+    from_right, _ = sub_side((zero, unit), p_saved, p_steps)
+    group = xlo * Y_SIZE
+    for k in range(2):
+        value = at_row(from_left[k], group) * y_side[0] + at_row(from_right[k], group) * y_side[1]
+        for t in range(2):
+            part_ref[pl.ds(2 * k + t, 1), :] = value[t, 0:1]
+    pl.semaphore_wait(ready, len(z_peers))
+    part_copies = [
+        pltpu.make_async_remote_copy(
+            src_ref=part_ref, dst_ref=parts_ref.at[yd], send_sem=part_send, recv_sem=part_recv,
+            device_id={"xg": xg, "yd": h * (Z_SIZE * Y_SIZE) + start + y}, device_id_type=MESH,
+        )
+        for start in plane_starts
+        for h in range(XLO_SIZE)
+        for y in range(Y_SIZE)
+    ]
+    for copy in part_copies:
+        copy.start()
+    for h in range(XLO_SIZE):
+        parts_ref[pl.ds(h * (Z_SIZE * Y_SIZE) + zz * Y_SIZE, Y_SIZE)] = jnp.zeros((Y_SIZE, 4, LANES), jnp.float32)
+
+    for copy in zc_copies:
+        copy.wait_recv()
+
+    def z_rows(ref, k):
+        width = ref.shape[1]
+        flat = ref.reshape(Z_SIZE * width, LANES)
+        return jnp.stack(
+            [
+                jnp.stack([flat[pl.ds(width // 2 * h + 2 * k + t, Z_SIZE, stride=width), :] for t in range(2)])
+                for h in range(2)
+            ]
+        )
+
+    z_coef, z_saved = sub_coef([z_rows(zc_ref, k) for k in range(3)], steps)
+    z_ring = ring_coef([value[0] for value in z_coef], [value[1] for value in z_coef])
+
     for copy in pr_copies:
-        copy.wait()
+        copy.wait_recv()
     p_side, p_mid = sub_side([plane_rows(pr_ref, k) for k in range(2)], p_saved, p_steps)
-    r_base = pl.multiple_of(zz * 8, 8)
+
+    others = parts_ref.at[pl.ds(0, len(part_copies))]
+    pltpu.make_async_copy(others, others, part_recv).wait()
+    for h in range(2):
+        for z in range(Z_SIZE):
+            first = h * (Z_SIZE * Y_SIZE) + z * Y_SIZE
+            total = parts_ref[first] + parts_ref[first + 1] + (parts_ref[first + 2] + parts_ref[first + 3])
+            sums_ref[z, 4 * h : 4 * h + 4, :] = total
     for h in range(2):
         for k in range(2):
             for t in range(2):
-                zr_ref[pl.ds(r_base + 4 * h + 2 * k + t, 1), :] = p_side[k][t, 4 * h : 4 * h + 1]
-    zr_copies = sends(zr_ref, 8, zz, z_peers, zr_send, zr_recv)
-    for copy in zr_copies:
-        copy.start()
-
-    for copy in zc_copies:
-        copy.wait()
-
-    def z_rows(ref, stride, half_rows, k):
-        return jnp.stack(
-            [
-                jnp.stack([ref[pl.ds(half_rows * h + 2 * k + t, Z_SIZE, stride=stride), :] for t in range(2)])
-                for h in range(2)
-            ]
-        )
-
-    z_coef, z_saved = sub_coef([z_rows(zc_ref, 16, 8, k) for k in range(3)], steps)
-    z_ring = ring_coef([value[0] for value in z_coef], [value[1] for value in z_coef])
-
-    for copy in zr_copies:
-        copy.wait()
-    z_side, z_mid = sub_side([z_rows(zr_ref, 8, 4, k) for k in range(2)], z_saved, steps)
+                sums_ref[zz, pl.ds(4 * h + 2 * k + t, 1), :] = p_side[k][t, 4 * h : 4 * h + 1]
+    z_side, z_mid = sub_side([z_rows(sums_ref, k) for k in range(2)], z_saved, steps)
     u_p, u_q = ring_solve(z_ring, [value[0] for value in z_side], [value[1] for value in z_side])
 
     def spread(value):
         return jnp.broadcast_to(value[:, 0:1], value.shape)
-
-    def picked(u_left, u_right, place):
-        for i, value in enumerate((u_left, u_right)):
-            for t in range(2):
-                pick_ref[i, t] = value[t]
-        return tuple(
-            jnp.stack([pick_ref[i, t, pl.ds(place, SUB, stride=0), :] for t in range(2)]) for i in range(2)
-        )
 
     lower = xlo == 0
     u_p, u_q = spread(u_p), spread(u_q)
@@ -344,39 +372,47 @@
     own_saved = [tuple(jnp.where(lower, value[0], value[1]) for value in factors) for factors in z_saved]
     own_mid = [jnp.where(lower, value[0], value[1]) for value in z_mid]
     u_left, u_right = sub_back(own_saved, own_mid, steps, u_left, u_right)
-    u_left, u_right = picked(u_left, u_right, zz)
+    u_left, u_right = at_row(u_left, zz), at_row(u_right, zz)
     u_left, u_right = sub_back(p_saved, p_mid, p_steps, u_left, u_right)
-    u_left, u_right = picked(u_left, u_right, slot)
+    u_left, u_right = at_row(u_left, slot), at_row(u_right, slot)
     u_left, u_right = sub_back(ys_saved, ys_mid, steps, u_left, u_right)
     updated = chain_back(y_saved, y_mid, u_left, u_right)
     for v in range(8):
         for t in range(2):
             out_ref[pl.ds(2 * v + t, SUB, stride=16), :] = updated[v, t]
 
+    for copy in x_copies + pc_copies + pr_copies + zc_copies:
+        copy.wait_send()
+    pltpu.make_async_copy(others, others, part_send).wait()
+
 
 def local(mobile, dispersion_x, dispersion_y, capacity, immobile, exchange_rates, rate_shares):
     flat = [value.reshape(ROWS, LANES) for value in (mobile, dispersion_x, dispersion_y, capacity)]
     any_spec = pl.BlockSpec(memory_space=pl.ANY)
-    smem_spec = pl.BlockSpec(memory_space=pltpu.SMEM)
     square = pltpu.VMEM((ROWS, LANES), jnp.float32)
+    zones = pltpu.SMEM((4,), jnp.float32)
     dma = pltpu.SemaphoreType.DMA
     updated = pl.pallas_call(
         kernel,
         out_shape=jax.ShapeDtypeStruct((ROWS, LANES), jnp.float32),
-        in_specs=[any_spec] * 5 + [smem_spec] * 2,
+        in_specs=[any_spec] * 7,
         out_specs=pl.BlockSpec(memory_space=pltpu.VMEM),
         scratch_shapes=[
-            square, square, square, square, pltpu.VMEM((4 * ROWS, LANES), jnp.float32), square, square, square,
+            square, square, square, square, pltpu.VMEM((4 * ROWS, LANES), jnp.float32), zones, zones,
+            square, square, square,
             pltpu.VMEM((XG_SIZE, 8, LANES), jnp.float32),
-            pltpu.VMEM((PLANE * 8, LANES), jnp.float32),
-            pltpu.VMEM((PLANE * 8, LANES), jnp.float32),
-            pltpu.VMEM((Z_SIZE * 16, LANES), jnp.float32),
-            pltpu.VMEM((Z_SIZE * 8, LANES), jnp.float32),
-            pltpu.VMEM((2, 2, SUB, LANES), jnp.float32),
-            dma((5,)),
+            pltpu.VMEM((PLANE, 8, LANES), jnp.float32),
+            pltpu.VMEM((PLANE, 8, LANES), jnp.float32),
+            pltpu.VMEM((Z_SIZE, 16, LANES), jnp.float32),
+            pltpu.VMEM((4, LANES), jnp.float32),
+            pltpu.VMEM((PLANE * Z_SIZE, 4, LANES), jnp.float32),
+            pltpu.VMEM((Z_SIZE, 8, LANES), jnp.float32),
+            pltpu.VMEM((2, SUB, LANES), jnp.float32),
+            dma((7,)),
             dma((XG_SIZE - 1,)), dma((XG_SIZE - 1,)),
             dma((PLANE - 1,)), dma((PLANE - 1,)), dma((PLANE - 1,)), dma((PLANE - 1,)),
-            dma((Z_SIZE - 1,)), dma((Z_SIZE - 1,)), dma((Z_SIZE - 1,)), dma((Z_SIZE - 1,)),
+            dma((Z_SIZE - 1,)), dma((Z_SIZE - 1,)), dma(()), dma(()),
+            pltpu.SemaphoreType.REGULAR,
         ],
         compiler_params=pltpu.CompilerParams(collective_id=0, has_side_effects=True),
     )(*flat, immobile.reshape(4 * ROWS, LANES), exchange_rates, rate_shares)

time: 24.4 us -> 24 us (0.984)
  Pallas kernels: 22.7 us -> 22.3 us
    pallas_call x1, Pallas kernels: 22.7 us -> 22.3 us  [local(): pl.pallas_call(kernel, out_shape=jax.ShapeDtypeStruct((ROWS, LANES), jnp....]
where the time goes in v2:
time: 24 us; the launch traced here: 23.7 us
  Pallas kernels  22.3 us (93%)
  local copies, waits for them, and re-layouts  1.47 us (6%)
    pallas_call x1, Pallas kernels, local(): pl.pallas_call(kernel, out_shape=jax.ShapeDtypeStruct((ROWS, LANES), jnp....  22.3 us
    unnamed x1, local copies, waits for them, and re-layouts  1.47 us

profile of v2, /device:TPU:2, one launch (start us, length us, event | category | flops | bytes accessed | tf_op | source)
XLA Modules:
  0.0 23.7 jit_solution(1568938380013113494)
XLA Ops:
  0.0 22.3 %shard_map.73 = f32[128,128]{1,0:T(8,128)} custom-call(f32[128,128]{1,0:T(8,128)} %bitcast.8, f32[128,128]{1,0:T(8,128)} %bitcast.9, f32[128,128]{1,0:T(8,128)} %bitcast.10, f32[128,128]{1,0:T(8,128)} %bitcast.11, f32[512,128]{1,0:T(8,128)} %bitcast.7, f32[4]{0:T(128)} %rates_hbm.1, f32[4]{0:T(128)} %shares_hbm.1), custom_call_target="tpu_custom_call" | custom-call | tf_op jit(solution)/shard_map/pallas_call | solution.py:395
  22.3 1.5 %copy.10 = f32[64,1,256]{2,1,0:T(1,128)} copy(f32[64,1,256]{2,1,0:T(1,128)} %bitcast.6) | data formatting | bytes 131072

commit v3 on v2

--- a/solution.py
+++ b/solution.py
@@ -173,11 +173,21 @@
     for k in range(1, PLANE):
         other = (slot + k) % PLANE
         plane_peers.append({"xg": xg, "yd": (other // Y_SIZE) * (Z_SIZE * Y_SIZE) + zz * Y_SIZE + other % Y_SIZE})
-    plane_starts = [((zz + k) % Z_SIZE) * Y_SIZE for k in (4, 3, 5, 2, 6, 1, 7)]
-    z_peers = [{"xg": xg, "yd": xlo * (Z_SIZE * Y_SIZE) + start + yy} for start in plane_starts]
+    z_peers = [
+        {"xg": xg, "yd": xlo * (Z_SIZE * Y_SIZE) + ((zz + k) % Z_SIZE) * Y_SIZE + yy} for k in range(1, Z_SIZE)
+    ]
+    y_peers = [{"xg": xg, "yd": yd - yy + (yy + k) % Y_SIZE} for k in range(1, Y_SIZE)]
+    column = zz * XLO_SIZE + xlo
+    starts = []
+    for k in range(XLO_SIZE * Z_SIZE - 1):
+        other = jnp.where(column <= k, k + 1, k)
+        starts.append((other % XLO_SIZE) * (Z_SIZE * Y_SIZE) + (other // XLO_SIZE) * Y_SIZE)
     barrier = pltpu.get_barrier_semaphore()
     for peer in z_peers + plane_peers + x_peers:
         pl.semaphore_signal(barrier, inc=1, device_id=peer, device_id_type=MESH)
+
+    pc_ref[Y_SIZE:] = jnp.ones((Y_SIZE, 8, LANES), jnp.float32)
+    pr_ref[Y_SIZE:] = jnp.zeros((Y_SIZE, 8, LANES), jnp.float32)
 
     def sends(ref, position, peers, send_sem, recv_sem):
         part = ref.at[position]
@@ -209,7 +219,7 @@
     y_coef, ys_saved = sub_coef(y_coef, steps)
     for k in range(3):
         for t in range(2):
-            pc_ref[slot, pl.ds(2 * k + t, 1), :] = y_coef[k][t, 0:1]
+            pc_ref[yy, pl.ds(2 * k + t, 1), :] = y_coef[k][t, 0:1]
 
     loads[4].wait()
     work_ref[...] = jnp.transpose(dx_ref[...])
@@ -236,11 +246,52 @@
         )
         for k in range(1, XG_SIZE)
     ]
-    pc_copies = sends(pc_ref, slot, plane_peers, pc_send, pc_recv)
+    pc_copies = sends(pc_ref, yy, y_peers, pc_send, pc_recv)
     for copy in x_copies + pc_copies:
         copy.start()
     for peer in z_peers:
         pl.semaphore_signal(ready, inc=1, device_id=peer, device_id_type=MESH)
+
+    for copy in pc_copies:
+        copy.wait_recv()
+
+    def group_rows(ref, k):
+        flat = ref.reshape(SUB * 8, LANES)
+        return jnp.stack([flat[pl.ds(2 * k + t, SUB, stride=8), :] for t in range(2)])
+
+    def spread(value):
+        return jnp.broadcast_to(value[:, 0:1], value.shape)
+
+    def at_row(value, place):
+        for t in range(2):
+            pick_ref[t] = value[t]
+        return jnp.stack([pick_ref[t, pl.ds(place, SUB, stride=0), :] for t in range(2)])
+
+    p_steps = (1, 2)
+    p_coef, p_saved = sub_coef([group_rows(pc_ref, k) for k in range(3)], p_steps)
+    own = xlo * Z_SIZE + zz
+    for k in range(3):
+        for t in range(2):
+            zc_ref[own, pl.ds(2 * k + t, 1), :] = p_coef[k][t, 0:1]
+    pl.semaphore_wait(ready, len(z_peers))
+    zc_part = zc_ref.at[own, pl.ds(0, 6)]
+    zc_copies = [
+        pltpu.make_async_remote_copy(
+            src_ref=zc_part, dst_ref=zc_part, send_sem=zc_send, recv_sem=zc_recv,
+            device_id={"xg": xg, "yd": start + yy}, device_id_type=MESH,
+        )
+        for start in starts
+    ]
+    for copy in zc_copies:
+        copy.start()
+
+    place = lax.broadcasted_iota(jnp.int32, (2, SUB, LANES), 1)
+    unit = jnp.where(place == yy, 1.0, 0.0)
+    zero = jnp.zeros_like(unit)
+    from_left, _ = sub_side((unit, zero), p_saved, p_steps)
+    from_right, _ = sub_side((zero, unit), p_saved, p_steps)
+    from_left = [spread(value) for value in from_left]
+    from_right = [spread(value) for value in from_right]
 
     for copy in x_copies:
         copy.wait_recv()
@@ -277,77 +328,43 @@
     y_side, ys_mid = sub_side(y_side, ys_saved, steps)
     for k in range(2):
         for t in range(2):
-            pr_ref[slot, pl.ds(2 * k + t, 1), :] = y_side[k][t, 0:1]
-    pr_copies = sends(pr_ref, slot, plane_peers, pr_send, pr_recv)
-    for copy in pr_copies:
-        copy.start()
-
-    for copy in pc_copies:
-        copy.wait_recv()
-
-    def plane_rows(ref, k):
-        flat = ref.reshape(PLANE * 8, LANES)
-        return jnp.stack([flat[pl.ds(2 * k + t, PLANE, stride=8), :] for t in range(2)])
-
-    def at_row(value, place):
-        for t in range(2):
-            pick_ref[t] = value[t]
-        return jnp.stack([pick_ref[t, pl.ds(place, SUB, stride=0), :] for t in range(2)])
-
-    p_steps = (1, 2)
-    p_coef, p_saved = sub_coef([plane_rows(pc_ref, k) for k in range(3)], p_steps)
-    for h in range(2):
-        for k in range(3):
-            for t in range(2):
-                zc_ref[zz, pl.ds(8 * h + 2 * k + t, 1), :] = p_coef[k][t, 4 * h : 4 * h + 1]
-    zc_copies = sends(zc_ref, zz, z_peers, zc_send, zc_recv)
-    for copy in zc_copies:
-        copy.start()
-
-    place = lax.broadcasted_iota(jnp.int32, (2, SUB, LANES), 1)
-    unit = jnp.where(place == slot, 1.0, 0.0)
-    zero = jnp.zeros_like(unit)
-    from_left, _ = sub_side((unit, zero), p_saved, p_steps)
-    from_right, _ = sub_side((zero, unit), p_saved, p_steps)
-    group = xlo * Y_SIZE
+            pr_ref[yy, pl.ds(2 * k + t, 1), :] = y_side[k][t, 0:1]
+    pr_copies = sends(pr_ref, yy, y_peers, pr_send, pr_recv)
+
     for k in range(2):
-        value = at_row(from_left[k], group) * y_side[0] + at_row(from_right[k], group) * y_side[1]
+        value = from_left[k] * y_side[0] + from_right[k] * y_side[1]
         for t in range(2):
             part_ref[pl.ds(2 * k + t, 1), :] = value[t, 0:1]
-    pl.semaphore_wait(ready, len(z_peers))
     part_copies = [
         pltpu.make_async_remote_copy(
             src_ref=part_ref, dst_ref=parts_ref.at[yd], send_sem=part_send, recv_sem=part_recv,
-            device_id={"xg": xg, "yd": h * (Z_SIZE * Y_SIZE) + start + y}, device_id_type=MESH,
-        )
-        for start in plane_starts
-        for h in range(XLO_SIZE)
+            device_id={"xg": xg, "yd": start + y}, device_id_type=MESH,
+        )
+        for start in starts
         for y in range(Y_SIZE)
     ]
-    for copy in part_copies:
+    for copy in part_copies + pr_copies:
         copy.start()
-    for h in range(XLO_SIZE):
-        parts_ref[pl.ds(h * (Z_SIZE * Y_SIZE) + zz * Y_SIZE, Y_SIZE)] = jnp.zeros((Y_SIZE, 4, LANES), jnp.float32)
-
-    for copy in zc_copies:
-        copy.wait_recv()
-
-    def z_rows(ref, k):
-        width = ref.shape[1]
-        flat = ref.reshape(Z_SIZE * width, LANES)
+    parts_ref[pl.ds(yd - yy, Y_SIZE)] = jnp.zeros((Y_SIZE, 4, LANES), jnp.float32)
+
+    other_coef = zc_ref.at[pl.ds(0, len(zc_copies)), pl.ds(0, 6)]
+    pltpu.make_async_copy(other_coef, other_coef, zc_recv).wait()
+
+    def z_rows(ref, half, k):
+        flat = ref.reshape(ref.shape[0] * 8, LANES)
         return jnp.stack(
             [
-                jnp.stack([flat[pl.ds(width // 2 * h + 2 * k + t, Z_SIZE, stride=width), :] for t in range(2)])
+                jnp.stack([flat[pl.ds(half * h + 2 * k + t, Z_SIZE, stride=8), :] for t in range(2)])
                 for h in range(2)
             ]
         )
 
-    z_coef, z_saved = sub_coef([z_rows(zc_ref, k) for k in range(3)], steps)
+    z_coef, z_saved = sub_coef([z_rows(zc_ref, 8 * Z_SIZE, k) for k in range(3)], steps)
     z_ring = ring_coef([value[0] for value in z_coef], [value[1] for value in z_coef])
 
     for copy in pr_copies:
         copy.wait_recv()
-    p_side, p_mid = sub_side([plane_rows(pr_ref, k) for k in range(2)], p_saved, p_steps)
+    p_side, p_mid = sub_side([group_rows(pr_ref, k) for k in range(2)], p_saved, p_steps)
 
     others = parts_ref.at[pl.ds(0, len(part_copies))]
     pltpu.make_async_copy(others, others, part_recv).wait()
@@ -356,15 +373,11 @@
             first = h * (Z_SIZE * Y_SIZE) + z * Y_SIZE
             total = parts_ref[first] + parts_ref[first + 1] + (parts_ref[first + 2] + parts_ref[first + 3])
             sums_ref[z, 4 * h : 4 * h + 4, :] = total
-    for h in range(2):
-        for k in range(2):
-            for t in range(2):
-                sums_ref[zz, pl.ds(4 * h + 2 * k + t, 1), :] = p_side[k][t, 4 * h : 4 * h + 1]
-    z_side, z_mid = sub_side([z_rows(sums_ref, k) for k in range(2)], z_saved, steps)
+    for k in range(2):
+        for t in range(2):
+            sums_ref[zz, pl.ds(4 * xlo + 2 * k + t, 1), :] = p_side[k][t, 0:1]
+    z_side, z_mid = sub_side([z_rows(sums_ref, 4, k) for k in range(2)], z_saved, steps)
     u_p, u_q = ring_solve(z_ring, [value[0] for value in z_side], [value[1] for value in z_side])
-
-    def spread(value):
-        return jnp.broadcast_to(value[:, 0:1], value.shape)
 
     lower = xlo == 0
     u_p, u_q = spread(u_p), spread(u_q)
@@ -374,15 +387,16 @@
     u_left, u_right = sub_back(own_saved, own_mid, steps, u_left, u_right)
     u_left, u_right = at_row(u_left, zz), at_row(u_right, zz)
     u_left, u_right = sub_back(p_saved, p_mid, p_steps, u_left, u_right)
-    u_left, u_right = at_row(u_left, slot), at_row(u_right, slot)
+    u_left, u_right = at_row(u_left, yy), at_row(u_right, yy)
     u_left, u_right = sub_back(ys_saved, ys_mid, steps, u_left, u_right)
     updated = chain_back(y_saved, y_mid, u_left, u_right)
     for v in range(8):
         for t in range(2):
             out_ref[pl.ds(2 * v + t, SUB, stride=16), :] = updated[v, t]
 
-    for copy in x_copies + pc_copies + pr_copies + zc_copies:
+    for copy in x_copies + pc_copies + pr_copies:
         copy.wait_send()
+    pltpu.make_async_copy(other_coef, other_coef, zc_send).wait()
     pltpu.make_async_copy(others, others, part_send).wait()
 
 
@@ -394,24 +408,24 @@
     dma = pltpu.SemaphoreType.DMA
     updated = pl.pallas_call(
         kernel,
-        out_shape=jax.ShapeDtypeStruct((ROWS, LANES), jnp.float32),
+        out_shape=pltpu.VMEM((ROWS, LANES), jnp.float32),
         in_specs=[any_spec] * 7,
         out_specs=pl.BlockSpec(memory_space=pltpu.VMEM),
         scratch_shapes=[
             square, square, square, square, pltpu.VMEM((4 * ROWS, LANES), jnp.float32), zones, zones,
             square, square, square,
             pltpu.VMEM((XG_SIZE, 8, LANES), jnp.float32),
-            pltpu.VMEM((PLANE, 8, LANES), jnp.float32),
-            pltpu.VMEM((PLANE, 8, LANES), jnp.float32),
-            pltpu.VMEM((Z_SIZE, 16, LANES), jnp.float32),
+            pltpu.VMEM((SUB, 8, LANES), jnp.float32),
+            pltpu.VMEM((SUB, 8, LANES), jnp.float32),
+            pltpu.VMEM((XLO_SIZE * Z_SIZE, 8, LANES), jnp.float32),
             pltpu.VMEM((4, LANES), jnp.float32),
             pltpu.VMEM((PLANE * Z_SIZE, 4, LANES), jnp.float32),
             pltpu.VMEM((Z_SIZE, 8, LANES), jnp.float32),
             pltpu.VMEM((2, SUB, LANES), jnp.float32),
             dma((7,)),
             dma((XG_SIZE - 1,)), dma((XG_SIZE - 1,)),
-            dma((PLANE - 1,)), dma((PLANE - 1,)), dma((PLANE - 1,)), dma((PLANE - 1,)),
-            dma((Z_SIZE - 1,)), dma((Z_SIZE - 1,)), dma(()), dma(()),
+            dma((Y_SIZE - 1,)), dma((Y_SIZE - 1,)), dma((Y_SIZE - 1,)), dma((Y_SIZE - 1,)),
+            dma(()), dma(()), dma(()), dma(()),
             pltpu.SemaphoreType.REGULAR,
         ],
         compiler_params=pltpu.CompilerParams(collective_id=0, has_side_effects=True),

time: 24 us -> 20 us (0.83)
  Pallas kernels: 22.3 us -> 19.3 us
  local copies, waits for them, and re-layouts: 1.47 us -> 0.63 us
    pallas_call x1, Pallas kernels: 22.3 us -> 19.3 us  [local(): pl.pallas_call(kernel, out_shape=pltpu.VMEM((ROWS, LANES), jnp.float32),...]
    unnamed x1, local copies, waits for them, and re-layouts: 1.47 us -> 0.63 us
where the time goes in v3:
time: 20 us
  Pallas kernels  19.3 us (96%)
  local copies, waits for them, and re-layouts  0.63 us (3%)
    pallas_call x1, Pallas kernels, local(): pl.pallas_call(kernel, out_shape=pltpu.VMEM((ROWS, LANES), jnp.float32),...  19.3 us
    unnamed x1, local copies, waits for them, and re-layouts  0.63 us

profile of v3, /device:TPU:2, one launch (start us, length us, event | category | flops | bytes accessed | tf_op | source)
XLA Modules:
  0.0 20.0 jit_solution(12891288937576513590)
XLA Ops:
  0.0 19.3 %shard_map.73 = f32[128,128]{1,0:T(8,128)S(1)} custom-call(f32[128,128]{1,0:T(8,128)} %bitcast.8, f32[128,128]{1,0:T(8,128)} %bitcast.9, f32[128,128]{1,0:T(8,128)} %bitcast.10, f32[128,128]{1,0:T(8,128)} %bitcast.11, f32[512,128]{1,0:T(8,128)} %bitcast.7, f32[4]{0:T(128)} %rates_hbm.1, f32[4]{0:T(128)} %shares_hbm.1), custom_call_target="tpu_custom_call" | custom-call | tf_op jit(solution)/shard_map/pallas_call | solution.py:409
  19.3 0.6 %copy.10 = f32[64,1,256]{2,1,0:T(1,128)} copy(f32[64,1,256]{2,1,0:T(1,128)S(1)} %bitcast.6) | data formatting | bytes 131072

commit v4 on v3

--- a/solution.py
+++ b/solution.py
@@ -35,7 +35,8 @@
 
 def between(factors, middle, u_left, u_right):
     a, b, inverse = factors
-    return middle * inverse + a * u_left + b * u_right
+    carried = a * u_left + b * u_right
+    return carried if middle is None else middle * inverse + carried
 
 
 def halves(values):
@@ -145,7 +146,7 @@
 def kernel(
     mobile_hbm, dx_hbm, dy_hbm, cap_hbm, imm_hbm, rates_hbm, shares_hbm, out_ref,
     mobile_ref, dx_ref, dy_ref, cap_ref, imm_ref, rates_ref, shares_ref, sto_ref, work_ref, work2_ref,
-    x_ref, pc_ref, pr_ref, zc_ref, part_ref, parts_ref, sums_ref, pick_ref,
+    x_ref, pc_ref, pr_ref, zc_ref, part_ref, parts_ref, sums_ref, pick_ref, res_ref,
     in_sem, x_send, x_recv, pc_send, pc_recv, pr_send, pr_recv,
     zc_send, zc_recv, part_send, part_recv, ready,
 ):
@@ -165,26 +166,32 @@
             ]
         )
     ]
+
+    def turned(position, steps, size):
+        return jnp.where(position >= size - steps, steps - size, steps)
+
+    across = jnp.where(xlo == 0, Z_SIZE * Y_SIZE, -Z_SIZE * Y_SIZE)
+    y_turns = [turned(yy, k, Y_SIZE) for k in range(1, Y_SIZE)]
+    x_peers = [{"xg": xg + turned(xg, k, XG_SIZE), "yd": yd} for k in range(1, XG_SIZE)]
+    y_peers = [{"xg": xg, "yd": yd + turn} for turn in y_turns]
+    plane_peers = y_peers + [{"xg": xg, "yd": yd + across + turn} for turn in [0] + y_turns]
+    z_turns = [turned(zz, k, Z_SIZE) * Y_SIZE for k in range(Z_SIZE)]
+    z_twos = [{"xg": xg, "yd": yd + z_turns[k]} for k in (2, Z_SIZE - 2)]
+    z_near = z_twos + [{"xg": xg, "yd": yd + z_turns[k]} for k in (1, Z_SIZE - 1)]
+    entered = plane_peers[::-1] + x_peers + z_near
+    barrier = pltpu.get_barrier_semaphore()
+
+    @pl.when(yd >= 0)
+    def _():
+        for peer in entered:
+            pl.semaphore_signal(barrier, inc=1, device_id=peer, device_id_type=MESH)
+
     for load in loads:
         load.start()
 
-    x_peers = [{"xg": (xg + k) % XG_SIZE, "yd": yd} for k in range(1, XG_SIZE)]
-    plane_peers = []
-    for k in range(1, PLANE):
-        other = (slot + k) % PLANE
-        plane_peers.append({"xg": xg, "yd": (other // Y_SIZE) * (Z_SIZE * Y_SIZE) + zz * Y_SIZE + other % Y_SIZE})
-    z_peers = [
-        {"xg": xg, "yd": xlo * (Z_SIZE * Y_SIZE) + ((zz + k) % Z_SIZE) * Y_SIZE + yy} for k in range(1, Z_SIZE)
-    ]
-    y_peers = [{"xg": xg, "yd": yd - yy + (yy + k) % Y_SIZE} for k in range(1, Y_SIZE)]
+    firsts = [h * (Z_SIZE * Y_SIZE) + z * Y_SIZE for z in range(Z_SIZE) for h in range(XLO_SIZE)]
     column = zz * XLO_SIZE + xlo
-    starts = []
-    for k in range(XLO_SIZE * Z_SIZE - 1):
-        other = jnp.where(column <= k, k + 1, k)
-        starts.append((other % XLO_SIZE) * (Z_SIZE * Y_SIZE) + (other // XLO_SIZE) * Y_SIZE)
-    barrier = pltpu.get_barrier_semaphore()
-    for peer in z_peers + plane_peers + x_peers:
-        pl.semaphore_signal(barrier, inc=1, device_id=peer, device_id_type=MESH)
+    starts = [jnp.where(column <= k, firsts[k + 1], firsts[k]) for k in range(len(firsts) - 1)]
 
     pc_ref[Y_SIZE:] = jnp.ones((Y_SIZE, 8, LANES), jnp.float32)
     pr_ref[Y_SIZE:] = jnp.zeros((Y_SIZE, 8, LANES), jnp.float32)
@@ -234,10 +241,24 @@
     x_side, x_mid = chain_side(strided(work_ref, 16), x_saved)
     x_coef, xs_saved = sub_coef(x_coef, steps)
     x_side, xs_mid = sub_side(x_side, xs_saved, steps)
-    for k, value in enumerate(x_coef + x_side):
+
+    def next_lane(value):
+        return roll(value, LANES - 1, 1)
+
+    even = (lax.broadcasted_iota(jnp.int32, (SUB, LANES), 1) & 1) == 0
+
+    def both_lanes(value):
+        value = jnp.where(even, value, roll(value, 1, 1))
+        return jnp.broadcast_to(value[0:1], (SUB, LANES))
+
+    own_coef, half_factors = join_coef(x_coef, [next_lane(value) for value in x_coef])
+    own_side, half_middle = join_side(x_side, [next_lane(value) for value in x_side], half_factors)
+    own_coef = [both_lanes(value) for value in own_coef]
+    own_side = [both_lanes(value) for value in own_side]
+    for k, value in enumerate(own_coef + own_side):
         x_ref[0, pl.ds(k, 1), :] = value[0:1]
 
-    pl.semaphore_wait(barrier, len(z_peers + plane_peers + x_peers))
+    pl.semaphore_wait(barrier, len(entered))
 
     x_copies = [
         pltpu.make_async_remote_copy(
@@ -249,8 +270,40 @@
     pc_copies = sends(pc_ref, yy, y_peers, pc_send, pc_recv)
     for copy in x_copies + pc_copies:
         copy.start()
-    for peer in z_peers:
-        pl.semaphore_signal(ready, inc=1, device_id=peer, device_id_type=MESH)
+    for peer in z_near:
+        pl.semaphore_signal(ready.at[0], inc=1, device_id=peer, device_id_type=MESH)
+    pl.semaphore_wait(ready.at[0], len(z_near))
+    for peer in z_twos:
+        pl.semaphore_signal(ready.at[1], inc=1, device_id=peer, device_id_type=MESH)
+
+    one = jnp.ones((SUB, LANES), jnp.float32)
+    none = jnp.zeros((SUB, LANES), jnp.float32)
+
+    def responses(saved, subs, middles, sub_middles, u_left, u_right, out):
+        u_left, u_right = sub_back(subs, sub_middles, steps, u_left, u_right)
+        cells = chain_back(saved, middles, u_left, u_right).reshape(16, SUB, LANES)
+        for v in range(16):
+            out[pl.ds(v, SUB, stride=16), :] = cells[v]
+        return out[...]
+
+    no_mid = [None] * len(x_mid)
+    no_sub = [None] * len(steps)
+    still = responses(x_saved, xs_saved, x_mid, xs_mid, none, none, work_ref)
+    by_left = responses(x_saved, xs_saved, no_mid, no_sub, one, none, work2_ref)
+    by_right = responses(x_saved, xs_saved, no_mid, no_sub, none, one, res_ref.at[0])
+    half_still = both_lanes(half_middle * half_factors[2])[0:1]
+    half_before = both_lanes(half_factors[0])[0:1]
+    half_last = both_lanes(half_factors[1])[0:1]
+    first = even[0:1]
+    res_ref[0] = still + jnp.where(first, by_right, by_left) * half_still
+    res_ref[1] = jnp.where(first, by_left + by_right * half_before, by_left * half_before)
+    res_ref[2] = jnp.where(first, by_right * half_last, by_right + by_left * half_last)
+
+    both = jnp.ones((2, SUB, LANES), jnp.float32)
+    neither = jnp.zeros((2, SUB, LANES), jnp.float32)
+    no_mid = [None] * len(y_saved)
+    res_ref[3] = responses(y_saved, ys_saved, no_mid, no_sub, both, neither, work_ref) * sto_ref[...]
+    res_ref[4] = responses(y_saved, ys_saved, no_mid, no_sub, neither, both, work2_ref) * sto_ref[...]
 
     for copy in pc_copies:
         copy.wait_recv()
@@ -273,16 +326,17 @@
     for k in range(3):
         for t in range(2):
             zc_ref[own, pl.ds(2 * k + t, 1), :] = p_coef[k][t, 0:1]
-    pl.semaphore_wait(ready, len(z_peers))
     zc_part = zc_ref.at[own, pl.ds(0, 6)]
+    zc_places = [yd - zz * Y_SIZE + jnp.where(zz <= k, k + 1, k) * Y_SIZE for k in range(Z_SIZE - 1)]
+    zc_places += [yd + across + z_turns[k] for k in (0, 1, 7, 2, 6, 3, 5, 4)]
     zc_copies = [
         pltpu.make_async_remote_copy(
             src_ref=zc_part, dst_ref=zc_part, send_sem=zc_send, recv_sem=zc_recv,
-            device_id={"xg": xg, "yd": start + yy}, device_id_type=MESH,
-        )
-        for start in starts
+            device_id={"xg": xg, "yd": place}, device_id_type=MESH,
+        )
+        for place in zc_places
     ]
-    for copy in zc_copies:
+    for copy in zc_copies[:-3]:
         copy.start()
 
     place = lax.broadcasted_iota(jnp.int32, (2, SUB, LANES), 1)
@@ -290,62 +344,62 @@
     zero = jnp.zeros_like(unit)
     from_left, _ = sub_side((unit, zero), p_saved, p_steps)
     from_right, _ = sub_side((zero, unit), p_saved, p_steps)
-    from_left = [spread(value) for value in from_left]
-    from_right = [spread(value) for value in from_right]
+    row = lax.broadcasted_iota(jnp.int32, (SUB, LANES), 0)
+
+    def in_rows(pair):
+        (a, b), (c, d) = [spread(value) for value in pair]
+        return jnp.where(row == 0, a, jnp.where(row == 1, b, jnp.where(row == 2, c, d)))
+
+    from_left = in_rows(from_left)
+    from_right = in_rows(from_right)
 
     for copy in x_copies:
         copy.wait_recv()
 
-    def next_lane(value):
-        return roll(value, LANES - 1, 1)
-
     def block(g):
-        rows = [x_ref[g, pl.ds(k, 1), :] for k in range(5)]
-        rows = [jnp.broadcast_to(row, (SUB, LANES)) for row in rows]
-        later = [next_lane(row) for row in rows]
-        coef, factors = join_coef(rows[:3], later[:3])
-        side, middle = join_side(rows[3:], later[3:], factors)
-        return coef, side, factors, middle
-
-    own_coef, own_side, own_factors, own_middle = block(0)
-    rest_coef, rest_side, _, _ = block(1)
+        rows = [jnp.broadcast_to(x_ref[g, pl.ds(k, 1), :], (SUB, LANES)) for k in range(5)]
+        return rows[:3], rows[3:]
+
+    rest_coef, rest_side = block(1)
     for g in (2, 3):
-        coef, side, _, _ = block(g)
+        coef, side = block(g)
         rest_coef, factors = join_coef(rest_coef, coef)
         rest_side, _ = join_side(rest_side, side, factors)
     u_before, u_last = ring_solve(ring_coef(own_coef, rest_coef), own_side, rest_side)
-    u_half = between(own_factors, own_middle, u_before, u_last)
-    even = (lax.broadcasted_iota(jnp.int32, (SUB, LANES), 1) & 1) == 0
-    u_left = jnp.where(even, u_before, roll(u_half, 1, 1))
-    u_right = jnp.where(even, u_half, roll(u_last, 1, 1))
-    u_left, u_right = sub_back(xs_saved, xs_mid, steps, u_left, u_right)
-    after_x = chain_back(x_saved, x_mid, u_left, u_right)
-    for v in range(16):
-        work_ref[pl.ds(v, SUB, stride=16), :] = after_x[v]
-    work2_ref[...] = jnp.transpose(work_ref[...]) * sto_ref[...]
-
-    y_side, y_mid = chain_side(strided(work2_ref, 16).reshape(8, 2, SUB, LANES), y_saved)
-    y_side, ys_mid = sub_side(y_side, ys_saved, steps)
-    for k in range(2):
-        for t in range(2):
-            pr_ref[yy, pl.ds(2 * k + t, 1), :] = y_side[k][t, 0:1]
+    after_x = jnp.transpose(res_ref[0] + res_ref[1] * u_before[0:1] + res_ref[2] * u_last[0:1])
+
+    def total(weights):
+        terms = (weights * after_x).reshape(16, SUB, LANES)
+        while terms.shape[0] > 1:
+            low, high = halves(terms)
+            terms = low + high
+        terms = terms[0] + roll(terms[0], 4, 0)
+        return terms + roll(terms, 2, 0)
+
+    f_left, f_right = total(res_ref[3]), total(res_ref[4])
+    part_ref[...] = (from_left * f_left + from_right * f_right)[0:4]
+    pr_ref[yy] = jnp.where(row < 2, f_left, f_right)
     pr_copies = sends(pr_ref, yy, y_peers, pr_send, pr_recv)
-
-    for k in range(2):
-        value = from_left[k] * y_side[0] + from_right[k] * y_side[1]
-        for t in range(2):
-            part_ref[pl.ds(2 * k + t, 1), :] = value[t, 0:1]
     part_copies = [
         pltpu.make_async_remote_copy(
             src_ref=part_ref, dst_ref=parts_ref.at[yd], send_sem=part_send, recv_sem=part_recv,
-            device_id={"xg": xg, "yd": start + y}, device_id_type=MESH,
-        )
-        for start in starts
-        for y in range(Y_SIZE)
+            device_id={"xg": xg, "yd": starts[k] + y}, device_id_type=MESH,
+        )
+        for k, y in sorted(
+            ((k, y) for k in range(len(starts)) for y in range(Y_SIZE)),
+            key=lambda place: (place[0] // 2 >= 4, min(place[1], 2), place),
+        )
     ]
-    for copy in part_copies + pr_copies:
+    for copy in pr_copies:
+        copy.start()
+    pl.semaphore_wait(ready.at[1], len(z_twos))
+    for copy in zc_copies[-3:] + part_copies:
         copy.start()
     parts_ref[pl.ds(yd - yy, Y_SIZE)] = jnp.zeros((Y_SIZE, 4, LANES), jnp.float32)
+
+    work_ref[...] = after_x * sto_ref[...]
+    y_side, y_mid = chain_side(strided(work_ref, 16).reshape(8, 2, SUB, LANES), y_saved)
+    _, ys_mid = sub_side(y_side, ys_saved, steps)
 
     other_coef = zc_ref.at[pl.ds(0, len(zc_copies)), pl.ds(0, 6)]
     pltpu.make_async_copy(other_coef, other_coef, zc_recv).wait()
@@ -422,11 +476,12 @@
             pltpu.VMEM((PLANE * Z_SIZE, 4, LANES), jnp.float32),
             pltpu.VMEM((Z_SIZE, 8, LANES), jnp.float32),
             pltpu.VMEM((2, SUB, LANES), jnp.float32),
+            pltpu.VMEM((5, ROWS, LANES), jnp.float32),
             dma((7,)),
             dma((XG_SIZE - 1,)), dma((XG_SIZE - 1,)),
             dma((Y_SIZE - 1,)), dma((Y_SIZE - 1,)), dma((Y_SIZE - 1,)), dma((Y_SIZE - 1,)),
             dma(()), dma(()), dma(()), dma(()),
-            pltpu.SemaphoreType.REGULAR,
+            pltpu.SemaphoreType.REGULAR((2,)),
         ],
         compiler_params=pltpu.CompilerParams(collective_id=0, has_side_effects=True),
     )(*flat, immobile.reshape(4 * ROWS, LANES), exchange_rates, rate_shares)

time: 20 us -> 19.8 us (0.990)
    pallas_call x1, Pallas kernels: 19.3 us -> 19.1 us  [local(): pl.pallas_call(kernel, out_shape=pltpu.VMEM((ROWS, LANES), jnp.float32),...]
where the time goes in v4:
time: 19.8 us; the launch traced here: 19.7 us
  Pallas kernels  19.1 us (96%)
  local copies, waits for them, and re-layouts  0.63 us (3%)
    pallas_call x1, Pallas kernels, local(): pl.pallas_call(kernel, out_shape=pltpu.VMEM((ROWS, LANES), jnp.float32),...  19.1 us
    unnamed x1, local copies, waits for them, and re-layouts  0.63 us

profile of v4, /device:TPU:2, one launch (start us, length us, event | category | flops | bytes accessed | tf_op | source)
XLA Modules:
  0.0 19.7 jit_solution(9398996192654142279)
XLA Ops:
  0.0 19.1 %shard_map.73 = f32[128,128]{1,0:T(8,128)S(1)} custom-call(f32[128,128]{1,0:T(8,128)} %bitcast.8, f32[128,128]{1,0:T(8,128)} %bitcast.9, f32[128,128]{1,0:T(8,128)} %bitcast.10, f32[128,128]{1,0:T(8,128)} %bitcast.11, f32[512,128]{1,0:T(8,128)} %bitcast.7, f32[4]{0:T(128)} %rates_hbm.1, f32[4]{0:T(128)} %shares_hbm.1), custom_call_target="tpu_custom_call" | custom-call | tf_op jit(solution)/shard_map/pallas_call | solution.py:463
  19.1 0.6 %copy.10 = f32[64,1,256]{2,1,0:T(1,128)} copy(f32[64,1,256]{2,1,0:T(1,128)S(1)} %bitcast.6) | data formatting | bytes 131072

commit v5 on v4

--- a/solution.py
+++ b/solution.py
@@ -302,8 +302,10 @@
     both = jnp.ones((2, SUB, LANES), jnp.float32)
     neither = jnp.zeros((2, SUB, LANES), jnp.float32)
     no_mid = [None] * len(y_saved)
-    res_ref[3] = responses(y_saved, ys_saved, no_mid, no_sub, both, neither, work_ref) * sto_ref[...]
-    res_ref[4] = responses(y_saved, ys_saved, no_mid, no_sub, neither, both, work2_ref) * sto_ref[...]
+    res_ref[5] = responses(y_saved, ys_saved, no_mid, no_sub, both, neither, work_ref)
+    res_ref[6] = responses(y_saved, ys_saved, no_mid, no_sub, neither, both, work2_ref)
+    res_ref[3] = res_ref[5] * sto_ref[...]
+    res_ref[4] = res_ref[6] * sto_ref[...]
 
     for copy in pc_copies:
         copy.wait_recv()
@@ -336,7 +338,7 @@
         )
         for place in zc_places
     ]
-    for copy in zc_copies[:-3]:
+    for copy in zc_copies[:4] + zc_copies[7:-3]:
         copy.start()
 
     place = lax.broadcasted_iota(jnp.int32, (2, SUB, LANES), 1)
@@ -393,16 +395,14 @@
     for copy in pr_copies:
         copy.start()
     pl.semaphore_wait(ready.at[1], len(z_twos))
-    for copy in zc_copies[-3:] + part_copies:
+    for copy in zc_copies[-3:] + part_copies[:32] + zc_copies[4:7]:
         copy.start()
     parts_ref[pl.ds(yd - yy, Y_SIZE)] = jnp.zeros((Y_SIZE, 4, LANES), jnp.float32)
 
     work_ref[...] = after_x * sto_ref[...]
     y_side, y_mid = chain_side(strided(work_ref, 16).reshape(8, 2, SUB, LANES), y_saved)
     _, ys_mid = sub_side(y_side, ys_saved, steps)
-
-    other_coef = zc_ref.at[pl.ds(0, len(zc_copies)), pl.ds(0, 6)]
-    pltpu.make_async_copy(other_coef, other_coef, zc_recv).wait()
+    res_ref[7] = responses(y_saved, ys_saved, y_mid, ys_mid, neither, neither, work2_ref)
 
     def z_rows(ref, half, k):
         flat = ref.reshape(ref.shape[0] * 8, LANES)
@@ -413,12 +413,17 @@
             ]
         )
 
+    for copy in pr_copies:
+        copy.wait_recv()
+    for copy in part_copies[32:]:
+        copy.start()
+    p_side, p_mid = sub_side([group_rows(pr_ref, k) for k in range(2)], p_saved, p_steps)
+    other_coef = zc_ref.at[pl.ds(0, len(zc_copies)), pl.ds(0, 6)]
+    pltpu.make_async_copy(other_coef, other_coef, zc_recv).wait()
+
     z_coef, z_saved = sub_coef([z_rows(zc_ref, 8 * Z_SIZE, k) for k in range(3)], steps)
     z_ring = ring_coef([value[0] for value in z_coef], [value[1] for value in z_coef])
 
-    for copy in pr_copies:
-        copy.wait_recv()
-    p_side, p_mid = sub_side([group_rows(pr_ref, k) for k in range(2)], p_saved, p_steps)
 
     others = parts_ref.at[pl.ds(0, len(part_copies))]
     pltpu.make_async_copy(others, others, part_recv).wait()
@@ -442,11 +447,11 @@
     u_left, u_right = at_row(u_left, zz), at_row(u_right, zz)
     u_left, u_right = sub_back(p_saved, p_mid, p_steps, u_left, u_right)
     u_left, u_right = at_row(u_left, yy), at_row(u_right, yy)
-    u_left, u_right = sub_back(ys_saved, ys_mid, steps, u_left, u_right)
-    updated = chain_back(y_saved, y_mid, u_left, u_right)
-    for v in range(8):
-        for t in range(2):
-            out_ref[pl.ds(2 * v + t, SUB, stride=16), :] = updated[v, t]
+    lower_half = (row & 1) == 0
+    u_left = jnp.where(lower_half, u_left[0], u_left[1])
+    u_right = jnp.where(lower_half, u_right[0], u_right[1])
+    own, by_left, by_right = [res_ref[k].reshape(16, SUB, LANES) for k in (7, 5, 6)]
+    out_ref[...] = (own + by_left * u_left + by_right * u_right).reshape(ROWS, LANES)
 
     for copy in x_copies + pc_copies + pr_copies:
         copy.wait_send()
@@ -476,7 +481,7 @@
             pltpu.VMEM((PLANE * Z_SIZE, 4, LANES), jnp.float32),
             pltpu.VMEM((Z_SIZE, 8, LANES), jnp.float32),
             pltpu.VMEM((2, SUB, LANES), jnp.float32),
-            pltpu.VMEM((5, ROWS, LANES), jnp.float32),
+            pltpu.VMEM((8, ROWS, LANES), jnp.float32),
             dma((7,)),
             dma((XG_SIZE - 1,)), dma((XG_SIZE - 1,)),
             dma((Y_SIZE - 1,)), dma((Y_SIZE - 1,)), dma((Y_SIZE - 1,)), dma((Y_SIZE - 1,)),

time: 19.8 us -> 19.7 us (level)
  no operation moved by 1% of the time
where the time goes in v5:
time: 19.7 us; the launch traced here: 19.6 us
  Pallas kernels  19 us (96%)
  local copies, waits for them, and re-layouts  0.63 us (3%)
    pallas_call x1, Pallas kernels, local(): pl.pallas_call(kernel, out_shape=pltpu.VMEM((ROWS, LANES), jnp.float32),...  19 us
    unnamed x1, local copies, waits for them, and re-layouts  0.63 us

profile of v5, /device:TPU:2, one launch (start us, length us, event | category | flops | bytes accessed | tf_op | source)
XLA Modules:
  0.0 19.6 jit_solution(17597966844583315171)
XLA Ops:
  0.0 19.0 %shard_map.73 = f32[128,128]{1,0:T(8,128)S(1)} custom-call(f32[128,128]{1,0:T(8,128)} %bitcast.8, f32[128,128]{1,0:T(8,128)} %bitcast.9, f32[128,128]{1,0:T(8,128)} %bitcast.10, f32[128,128]{1,0:T(8,128)} %bitcast.11, f32[512,128]{1,0:T(8,128)} %bitcast.7, f32[4]{0:T(128)} %rates_hbm.1, f32[4]{0:T(128)} %shares_hbm.1), custom_call_target="tpu_custom_call" | custom-call | tf_op jit(solution)/shard_map/pallas_call | solution.py:468
  19.0 0.6 %copy.10 = f32[64,1,256]{2,1,0:T(1,128)} copy(f32[64,1,256]{2,1,0:T(1,128)S(1)} %bitcast.6) | data formatting | bytes 131072

commit v6 on v5

--- a/solution.py
+++ b/solution.py
@@ -389,7 +389,7 @@
         )
         for k, y in sorted(
             ((k, y) for k in range(len(starts)) for y in range(Y_SIZE)),
-            key=lambda place: (place[0] // 2 >= 4, min(place[1], 2), place),
+            key=lambda place: (place[0] // 2 >= 4, 60 * (place[0] // 2) + 75 * min(place[1], 2), place),
         )
     ]
     for copy in pr_copies:

time: 19.7 us -> 19.7 us (level)
  no operation moved by 1% of the time
where the time goes in v6:
time: 19.7 us; the launch traced here: 19.6 us
  Pallas kernels  19 us (96%)
  local copies, waits for them, and re-layouts  0.63 us (3%)
    pallas_call x1, Pallas kernels, local(): pl.pallas_call(kernel, out_shape=pltpu.VMEM((ROWS, LANES), jnp.float32),...  19 us
    unnamed x1, local copies, waits for them, and re-layouts  0.63 us

profile of v6, /device:TPU:2, one launch (start us, length us, event | category | flops | bytes accessed | tf_op | source)
XLA Modules:
  0.0 19.6 jit_solution(17476844713057148236)
XLA Ops:
  0.0 19.0 %shard_map.73 = f32[128,128]{1,0:T(8,128)S(1)} custom-call(f32[128,128]{1,0:T(8,128)} %bitcast.8, f32[128,128]{1,0:T(8,128)} %bitcast.9, f32[128,128]{1,0:T(8,128)} %bitcast.10, f32[128,128]{1,0:T(8,128)} %bitcast.11, f32[512,128]{1,0:T(8,128)} %bitcast.7, f32[4]{0:T(128)} %rates_hbm.1, f32[4]{0:T(128)} %shares_hbm.1), custom_call_target="tpu_custom_call" | custom-call | tf_op jit(solution)/shard_map/pallas_call | solution.py:468
  19.0 0.6 %copy.10 = f32[64,1,256]{2,1,0:T(1,128)} copy(f32[64,1,256]{2,1,0:T(1,128)S(1)} %bitcast.6) | data formatting | bytes 131072

commit v7 on v6

--- a/solution.py
+++ b/solution.py
@@ -389,7 +389,7 @@
         )
         for k, y in sorted(
             ((k, y) for k in range(len(starts)) for y in range(Y_SIZE)),
-            key=lambda place: (place[0] // 2 >= 4, 60 * (place[0] // 2) + 75 * min(place[1], 2), place),
+            key=lambda place: (place[0] // 2 >= 4, 40 * (place[0] // 2) + 75 * min(place[1], 2), place),
         )
     ]
     for copy in pr_copies:

time: 19.7 us -> 19.7 us (level)
  no operation moved by 1% of the time
where the time goes in v7:
time: 19.7 us; the launch traced here: 19.6 us
  Pallas kernels  19 us (96%)
  local copies, waits for them, and re-layouts  0.63 us (3%)
    pallas_call x1, Pallas kernels, local(): pl.pallas_call(kernel, out_shape=pltpu.VMEM((ROWS, LANES), jnp.float32),...  19 us
    unnamed x1, local copies, waits for them, and re-layouts  0.63 us

profile of v7, /device:TPU:2, one launch (start us, length us, event | category | flops | bytes accessed | tf_op | source)
XLA Modules:
  0.0 19.6 jit_solution(18400333200409784418)
XLA Ops:
  0.0 19.0 %shard_map.73 = f32[128,128]{1,0:T(8,128)S(1)} custom-call(f32[128,128]{1,0:T(8,128)} %bitcast.8, f32[128,128]{1,0:T(8,128)} %bitcast.9, f32[128,128]{1,0:T(8,128)} %bitcast.10, f32[128,128]{1,0:T(8,128)} %bitcast.11, f32[512,128]{1,0:T(8,128)} %bitcast.7, f32[4]{0:T(128)} %rates_hbm.1, f32[4]{0:T(128)} %shares_hbm.1), custom_call_target="tpu_custom_call" | custom-call | tf_op jit(solution)/shard_map/pallas_call | solution.py:468
  19.0 0.6 %copy.10 = f32[64,1,256]{2,1,0:T(1,128)} copy(f32[64,1,256]{2,1,0:T(1,128)S(1)} %bitcast.6) | data formatting | bytes 131072
